TPU v7x, 32 devices: a whole 2x2x4 slice. The times are simulated.
32 devices in a mesh: dp: 8 (over y, x, core), tensor: 4 (over z).
Axes of the slice: x: 2, y: 2, z: 4, core: 2. Of those that a mesh axis runs over, the one named last changes fastest.
Arguments:
- inputs: bfloat16 [18432, 768], P('dp'), may hold values from -6 to 6
- cotangent: bfloat16 [18432, 768], P('dp'), may hold values from -6 to 6, as said below
- row_expert: int32 [18432], P('dp'), may hold values from 0 to 2, as said below
- row_keep: int32 [18432], P('dp'), may hold values from 0 to 1, as said below
- window_resolution: int32 [24], P('dp'), may hold values from 0 to 1, as said below
- attention_norm_gain: float32 [768], replicated, may hold values from 0.5 to 1.5
- attention_norm_bias: float32 [768], replicated, may hold values from -0.6 to 0.6
- qkv_weight: bfloat16 [3, 768, 768], P(None, None, 'tensor'), may hold values from -0.21875 to 0.21875
- qv_bias: float32 [2, 12, 64], P(None, 'tensor'), may hold values from -1.8 to 1.8
- out_weight: bfloat16 [768, 768], P('tensor'), may hold values from -2.5 to 2.5
- out_bias: float32 [768], replicated, may hold values from -0.6 to 0.6
- second_gain: float32 [3, 768], replicated, may hold values from 0.5 to 1.5
- expert_norm_bias: float32 [3, 768], replicated, may hold values from -0.6 to 0.6
- up_weight: bfloat16 [3, 768, 3072], P(None, None, 'tensor'), may hold values from -0.21875 to 0.21875
- up_bias: float32 [3, 3072], P(None, 'tensor'), may hold values from -0.6 to 0.6
- down_weight: bfloat16 [3, 3072, 768], P(None, 'tensor'), may hold values from -0.109375 to 0.109375
- down_bias: float32 [3, 768], replicated, may hold values from -0.6 to 0.6
Outputs:
- layer_out: bfloat16 [18432, 768], P('dp')
- input_rows_gradient: bfloat16 [18432, 768], P('dp')
- attention_gain_gradient: float32 [768], replicated
- grad_first_bias: float32 [768], replicated
- grad_qkv: float32 [3, 768, 768], P(None, 'dp', 'tensor')
- grad_qv_bias: float32 [2, 12, 64], P(None, 'tensor')
- grad_out_weight: float32 [768, 768], P('tensor', 'dp')
- grad_out_bias: float32 [768], replicated
- expert_gain_gradient: float32 [3, 768], replicated
- grad_second_bias: float32 [3, 768], replicated
- grad_up: float32 [3, 768, 3072], P(None, 'dp', 'tensor')
- grad_up_bias: float32 [3, 3072], P(None, 'tensor')
- grad_down: float32 [3, 3072, 768], P(None, 'tensor', 'dp')
- grad_down_bias: float32 [3, 768], replicated
Inputs may be any that keep to these rules, and one draw needn't show every extreme that they name: `row_expert`: rows come in windows of 768 slots. A window with window_resolution = 1 holds one pair: 577 image rows, then 1 to 64 text rows, then padding. One with 0 holds two pairs, one in each half of 384 slots, each of 197 image rows, then 1 to 64 text rows, then padding. In some pairs every real row uses expert 2; otherwise image rows use 0 and text rows 1. Padding rows use 1. `row_keep`: 1 on the image and text rows of a pair, 0 on its padding; every pair has padding and its first row is real. `window_resolution`: all windows of one index of dp have the same value. `cotangent`: 0 on every row with row_keep = 0.
All inputs are finite; a program needn't handle non-finite values.
Results may differ from a plain program's by a relative error of at most 0.015.
Values may be sent and summed in bfloat16 or wider, within the bound.
No kernel may reach another device: no remote copies, remote signals or barrier semaphores. Data moves between devices by JAX's collectives and lax.ppermute only.
A program may use at most 256 MiB of HBM per device.

v0:
```python
import math

import jax
import jax.numpy as jnp
from jax import lax
from jax.sharding import PartitionSpec as P

HEAD_DIM = 64
S = 768
BLK = 128


epsilon = 1e-05
masked_score = -1000000000.0


def gelu_exact(values):
    return jax.nn.gelu(values, approximate=False)


def apply_layer_norm(values):
    mean_row = jnp.mean(values, -1, keepdims=True)
    centred = values - mean_row
    variance = jnp.mean(centred * centred, -1, keepdims=True)
    inverse_deviation = lax.rsqrt(variance + epsilon)
    return (centred * inverse_deviation, inverse_deviation)


def norm_backward_pass(rowwise_gradient, centred_normalized, inverse_deviation, rowwise_gain):
    scaled_output = rowwise_gradient * rowwise_gain
    return inverse_deviation * (
        scaled_output
        - jnp.mean(scaled_output, -1, keepdims=True)
        - centred_normalized * jnp.mean(scaled_output * centred_normalized, -1, keepdims=True)
    )


def lookup_table_rows(table, expert_selector_float):
    result = jnp.zeros((expert_selector_float.shape[0], table.shape[1]), jnp.float32)
    for expert_id in range(table.shape[0]):
        result = (
            result + expert_selector_float[:, expert_id : expert_id + 1] * table[expert_id][None, :]
        )
    return result


def grouped_totals(expert_selector_float, values):
    return jnp.einsum("re,rd->ed", expert_selector_float, values, precision=lax.Precision.HIGHEST)


def total_rows(values):
    return lax.psum(values, "tensor")


def group_slots(onehot_int, row_count):
    expert_count = onehot_int.shape[1]
    counts = jnp.sum(onehot_int, 0)
    padded = (counts + BLK - 1) // BLK * BLK
    group_ends = jnp.cumsum(padded)
    group_starts = group_ends - padded
    row_ranks = jnp.cumsum(onehot_int, 0) - onehot_int
    row_slots = jnp.sum(onehot_int * (group_starts[None, :] + row_ranks), 1)
    block_count = row_count // BLK + expert_count - 1
    sources = jnp.full((block_count * BLK,), row_count, jnp.int32)
    sources = sources.at[row_slots].set(jnp.arange(row_count, dtype=jnp.int32))
    firsts = jnp.arange(block_count, dtype=jnp.int32) * BLK
    block_expert = jnp.minimum(
        jnp.sum((firsts[:, None] >= group_ends[None, :]).astype(jnp.int32), 1), expert_count - 1
    )
    return (row_slots, sources, block_expert)


def head_split(rows_in):
    return rows_in.reshape(rows_in.shape[0], rows_in.shape[1] // HEAD_DIM, HEAD_DIM)


def masked_scores(q_heads, k_heads, keep_rows, single):
    scale_factor = 1.0 / math.sqrt(HEAD_DIM)
    scores = (
        jnp.einsum("qhd,khd->hqk", q_heads, k_heads, preferred_element_type=jnp.float32)
        * scale_factor
    )
    positions = jnp.arange(keep_rows.shape[0], dtype=jnp.int32)
    upper = positions >= keep_rows.shape[0] // 2
    same_half = upper[:, None] == upper[None, :]
    allowed = (keep_rows[None, :] > 0) & (same_half | (single > 0))
    return jnp.where(allowed[None, :, :], scores, masked_score)


def attend_forward(pieces):
    query_rows, key_rows, value_rows, keep_rows, single = pieces
    q_heads, k_heads, v_heads = (
        head_split(query_rows),
        head_split(key_rows),
        head_split(value_rows),
    )
    scores = masked_scores(q_heads, k_heads, keep_rows, single)
    row_max = jnp.max(scores, -1, keepdims=True)
    exp_scores = jnp.exp(scores - row_max)
    exp_total = jnp.sum(exp_scores, -1, keepdims=True)
    weights = (exp_scores / exp_total).astype(jnp.bfloat16)
    log_totals = row_max[..., 0] + jnp.log(exp_total[..., 0])
    mixed_heads = jnp.einsum("hqk,khd->qhd", weights, v_heads, preferred_element_type=jnp.float32)
    return (mixed_heads.astype(jnp.bfloat16).reshape(query_rows.shape), log_totals)


def attend_backward(pieces):
    query_rows, key_rows, value_rows, keep_rows, single, log_totals, rowwise_gradient = pieces
    scale_factor = 1.0 / math.sqrt(HEAD_DIM)
    q_heads, k_heads, v_heads = (
        head_split(query_rows),
        head_split(key_rows),
        head_split(value_rows),
    )
    grad_heads = head_split(rowwise_gradient)
    scores = masked_scores(q_heads, k_heads, keep_rows, single)
    probs = jnp.exp(scores - log_totals[..., None])
    weights = probs.astype(jnp.bfloat16)
    grad_value = jnp.einsum("hqk,qhd->khd", weights, grad_heads, preferred_element_type=jnp.float32)
    grad_probs = jnp.einsum("qhd,khd->hqk", grad_heads, v_heads, preferred_element_type=jnp.float32)
    grad_scores = probs * (grad_probs - jnp.sum(probs * grad_probs, -1, keepdims=True))
    grad_scores = grad_scores.astype(jnp.bfloat16)
    grad_query = (
        jnp.einsum("hqk,khd->qhd", grad_scores, k_heads, preferred_element_type=jnp.float32)
        * scale_factor
    )
    grad_key = (
        jnp.einsum("hqk,qhd->khd", grad_scores, q_heads, preferred_element_type=jnp.float32)
        * scale_factor
    )
    return (
        grad_query.astype(jnp.bfloat16).reshape(query_rows.shape),
        grad_key.astype(jnp.bfloat16).reshape(query_rows.shape),
        grad_value.astype(jnp.bfloat16).reshape(query_rows.shape),
    )


def body(
    inputs,
    cotangent,
    row_expert,
    row_keep,
    window_resolution,
    attention_norm_gain,
    attention_norm_bias,
    qkv_weight,
    qv_bias,
    out_weight,
    out_bias,
    second_gain,
    expert_norm_bias,
    up_weight,
    up_bias,
    down_weight,
    down_bias,
):
    row_count, model_width = inputs.shape
    expert_count = up_weight.shape[0]
    local_width = qkv_weight.shape[2]
    seq_count = row_count // S
    share_count = row_count // lax.axis_size("tensor")
    share_start = lax.axis_index("tensor") * share_count

    def local_row_block(values):
        return lax.dynamic_slice_in_dim(values, share_start, share_count, 0)

    gathered_source_rows = inputs.astype(jnp.float32)
    onehot_int = (row_expert[:, None] == jnp.arange(expert_count, dtype=jnp.int32)[None, :]).astype(
        jnp.int32
    )
    expert_selector_float = onehot_int.astype(jnp.float32)
    expert_selector_local = local_row_block(expert_selector_float)
    attention_centred, attention_inverse_deviation = apply_layer_norm(gathered_source_rows)
    attention_normed = (attention_centred * attention_norm_gain + attention_norm_bias).astype(
        jnp.bfloat16
    )
    bias_pair = qv_bias.reshape(2, local_width)
    query = (
        jnp.dot(attention_normed, qkv_weight[0], preferred_element_type=jnp.float32) + bias_pair[0]
    ).astype(jnp.bfloat16)
    keyed = jnp.dot(attention_normed, qkv_weight[1], preferred_element_type=jnp.float32).astype(
        jnp.bfloat16
    )
    valued = (
        jnp.dot(attention_normed, qkv_weight[2], preferred_element_type=jnp.float32) + bias_pair[1]
    ).astype(jnp.bfloat16)
    seq_query = query.reshape(seq_count, S, local_width)
    seq_key = keyed.reshape(seq_count, S, local_width)
    seq_value = valued.reshape(seq_count, S, local_width)
    seq_keep = row_keep.reshape(seq_count, S)
    mixed_seq, log_totals = lax.map(
        attend_forward, (seq_query, seq_key, seq_value, seq_keep, window_resolution)
    )
    mixed = mixed_seq.reshape(row_count, local_width)
    attn_part = jnp.dot(mixed, out_weight, preferred_element_type=jnp.float32)
    residual_hidden = gathered_source_rows + (total_rows(attn_part) + out_bias)
    expert_centred, expert_inverse_deviation = apply_layer_norm(residual_hidden)
    rowwise_gain = lookup_table_rows(second_gain, expert_selector_float)
    expert_normed = (
        expert_centred * rowwise_gain + lookup_table_rows(expert_norm_bias, expert_selector_float)
    ).astype(jnp.bfloat16)
    expert_centred_local = local_row_block(expert_centred)
    row_slots, sources, block_expert = group_slots(onehot_int, row_count)
    block_count = block_expert.shape[0]
    zero_row = jnp.zeros((1, model_width), jnp.bfloat16)
    hidden_in = jnp.concatenate([expert_normed, zero_row], 0)[sources].reshape(
        block_count, BLK, model_width
    )

    def expert_block(pieces):
        block_in, expert_id = pieces
        up_mat = lax.dynamic_index_in_dim(up_weight, expert_id, 0, keepdims=False)
        down_mat = lax.dynamic_index_in_dim(down_weight, expert_id, 0, keepdims=False)
        up_row = lax.dynamic_index_in_dim(up_bias, expert_id, 0, keepdims=False)
        pre_act = jnp.dot(block_in, up_mat, preferred_element_type=jnp.float32) + up_row
        act_out = gelu_exact(pre_act).astype(jnp.bfloat16)
        block_out = jnp.dot(act_out, down_mat, preferred_element_type=jnp.float32)
        return (pre_act, act_out, block_out)

    pre_blocks, act_blocks, out_blocks = lax.map(expert_block, (hidden_in, block_expert))
    expert_part = out_blocks.reshape(block_count * BLK, model_width)[row_slots]
    layer_out = (
        residual_hidden
        + (total_rows(expert_part) + lookup_table_rows(down_bias, expert_selector_float))
    ).astype(jnp.bfloat16)
    cot_own = local_row_block(cotangent).astype(jnp.float32)
    grad_down_bias = grouped_totals(expert_selector_local, cot_own)
    grad_in_blocks = jnp.concatenate([cotangent, zero_row], 0)[sources].reshape(
        block_count, BLK, model_width
    )

    def expert_back(running, pieces):
        acc_up, acc_down, acc_up_bias = running
        block_in, pre_act, act_out, grad_block, expert_id = pieces
        up_mat = lax.dynamic_index_in_dim(up_weight, expert_id, 0, keepdims=False)
        down_mat = lax.dynamic_index_in_dim(down_weight, expert_id, 0, keepdims=False)
        grad_act = jnp.einsum("rd,fd->rf", grad_block, down_mat, preferred_element_type=jnp.float32)
        _, pullback = jax.vjp(gelu_exact, pre_act)
        grad_pre = pullback(grad_act)[0].astype(jnp.bfloat16)
        acc_up = acc_up.at[expert_id].add(
            jnp.einsum("rd,rf->df", block_in, grad_pre, preferred_element_type=jnp.float32)
        )
        acc_down = acc_down.at[expert_id].add(
            jnp.einsum("rf,rd->fd", act_out, grad_block, preferred_element_type=jnp.float32)
        )
        acc_up_bias = acc_up_bias.at[expert_id].add(jnp.sum(grad_pre.astype(jnp.float32), 0))
        grad_hidden = jnp.einsum("rf,df->rd", grad_pre, up_mat, preferred_element_type=jnp.float32)
        return ((acc_up, acc_down, acc_up_bias), grad_hidden)

    start_state = (
        jnp.zeros(up_weight.shape, jnp.float32),
        jnp.zeros(down_weight.shape, jnp.float32),
        jnp.zeros(up_bias.shape, jnp.float32),
    )
    (grad_up, grad_down, grad_up_bias), grad_hidden_blocks = lax.scan(
        expert_back, start_state, (hidden_in, pre_blocks, act_blocks, grad_in_blocks, block_expert)
    )
    hidden_part = grad_hidden_blocks.reshape(block_count * BLK, model_width)[row_slots]
    expert_normed_gradient = total_rows(hidden_part)
    residual_gradient = cotangent.astype(jnp.float32) + norm_backward_pass(
        expert_normed_gradient, expert_centred, expert_inverse_deviation, rowwise_gain
    )
    grad_attn = residual_gradient.astype(jnp.bfloat16)
    expert_normed_gradient_local = local_row_block(expert_normed_gradient)
    grad_attn_own = local_row_block(grad_attn)
    expert_gain_gradient = grouped_totals(
        expert_selector_local, expert_normed_gradient_local * expert_centred_local
    )
    grad_second_bias = grouped_totals(expert_selector_local, expert_normed_gradient_local)
    grad_out_bias = jnp.sum(grad_attn_own.astype(jnp.float32), 0)
    grad_out_weight = jnp.einsum("rh,rd->hd", mixed, grad_attn, preferred_element_type=jnp.float32)
    grad_mixed = jnp.einsum(
        "rd,hd->rh", grad_attn, out_weight, preferred_element_type=jnp.float32
    ).astype(jnp.bfloat16)
    grad_q_seq, grad_k_seq, grad_v_seq = lax.map(
        attend_backward,
        (
            seq_query,
            seq_key,
            seq_value,
            seq_keep,
            window_resolution,
            log_totals,
            grad_mixed.reshape(seq_count, S, local_width),
        ),
    )
    grad_query = grad_q_seq.reshape(row_count, local_width)
    grad_key = grad_k_seq.reshape(row_count, local_width)
    grad_value = grad_v_seq.reshape(row_count, local_width)
    grad_qkv = jnp.stack(
        [
            jnp.einsum("rd,rh->dh", attention_normed, grad_part, preferred_element_type=jnp.float32)
            for grad_part in (grad_query, grad_key, grad_value)
        ]
    )
    grad_qv_bias = jnp.stack(
        [jnp.sum(grad_query.astype(jnp.float32), 0), jnp.sum(grad_value.astype(jnp.float32), 0)]
    ).reshape(qv_bias.shape)
    first_part = jnp.einsum(
        "rh,dh->rd", grad_query, qkv_weight[0], preferred_element_type=jnp.float32
    )
    first_part = first_part + jnp.einsum(
        "rh,dh->rd", grad_key, qkv_weight[1], preferred_element_type=jnp.float32
    )
    first_part = first_part + jnp.einsum(
        "rh,dh->rd", grad_value, qkv_weight[2], preferred_element_type=jnp.float32
    )
    attention_centred_local = local_row_block(attention_centred)
    attention_normed_gradient = total_rows(first_part)
    input_rows_gradient = (
        residual_gradient
        + norm_backward_pass(
            attention_normed_gradient,
            attention_centred,
            attention_inverse_deviation,
            attention_norm_gain,
        )
    ).astype(jnp.bfloat16)
    attention_normed_gradient_local = local_row_block(attention_normed_gradient)
    attention_gain_gradient = jnp.sum(attention_normed_gradient_local * attention_centred_local, 0)
    grad_first_bias = jnp.sum(attention_normed_gradient_local, 0)
    summed_qkv, summed_out, summed_up, summed_down = (
        lax.psum_scatter(
            grad_qkv.astype(jnp.bfloat16), "dp", scatter_dimension=1, tiled=True
        ).astype(jnp.float32),
        lax.psum_scatter(
            grad_out_weight.astype(jnp.bfloat16), "dp", scatter_dimension=1, tiled=True
        ).astype(jnp.float32),
        lax.psum_scatter(
            grad_up.astype(jnp.bfloat16), "dp", scatter_dimension=1, tiled=True
        ).astype(jnp.float32),
        lax.psum_scatter(
            grad_down.astype(jnp.bfloat16), "dp", scatter_dimension=2, tiled=True
        ).astype(jnp.float32),
    )
    norm_sums = lax.psum(
        (
            attention_gain_gradient,
            grad_first_bias,
            grad_out_bias,
            expert_gain_gradient,
            grad_second_bias,
            grad_down_bias,
        ),
        ("dp", "tensor"),
    )
    small_sums = lax.psum((grad_qv_bias, grad_up_bias), "dp")
    return (
        layer_out,
        input_rows_gradient,
        norm_sums[0],
        norm_sums[1],
        summed_qkv,
        small_sums[0],
        summed_out,
        norm_sums[2],
        norm_sums[3],
        norm_sums[4],
        summed_up,
        small_sums[1],
        summed_down,
        norm_sums[5],
    )


def solution(mesh):
    in_specs = (
        P("dp", None),
        P("dp", None),
        P("dp"),
        P("dp"),
        P("dp"),
        P(),
        P(),
        P(None, None, "tensor"),
        P(None, "tensor", None),
        P("tensor", None),
        P(),
        P(),
        P(),
        P(None, None, "tensor"),
        P(None, "tensor"),
        P(None, "tensor", None),
        P(),
    )
    out_specs = (
        P("dp", None),
        P("dp", None),
        P(),
        P(),
        P(None, "dp", "tensor"),
        P(None, "tensor", None),
        P("tensor", "dp"),
        P(),
        P(),
        P(),
        P(None, "dp", "tensor"),
        P(None, "tensor"),
        P(None, "tensor", "dp"),
        P(),
    )
    return jax.shard_map(body, mesh=mesh, in_specs=in_specs, out_specs=out_specs, check_vma=False)
```

profile of v0, /device:TPU:0, one launch (start us, length us, event | category | flops | bytes accessed | tf_op | source)
XLA Modules:
  0.0 2110.3 jit_solution(14729037549028274431)
XLA Ops:
  13.2 5.3 fusion.82
  26.8 26.4 %while.59 = (s32[]{:T(128)}, bf16[3,768,192]{1,2,0:T(8,128)(2,1)}, f32[3,3,768]{2,1,0:T(4,128)}, bf16[3,768,192]{1,2,0:T(8,128)(2,1)S(1)}, s32[3,768]{1,0:T(4,12...) while((s32[]{:T(128)}, bf16[3,768,192]{1,2,0:T(8,128)(2,1)}, ...), condition=%wide.region_5.6_spmd, body=%wide.region_2.5_spmd.sunk | while | flops 476134656 | bytes 27215000 | solution.py:191
  56.0 4.1 fusion.131
  61.8 4.0 concatenate.18
  66.1 9.0 scatter_custom_fusion
  75.1 13.0 gather_fusion.2
  89.1 222.3 %all-reduce.9.cloned.1.call-done = f32[2304,768]{1,0:T(8,128)} async-done(((f32[2304,768]{1,0:T(8,128)}), f32[2304,768]{1,0:T(8,128)}) %all-reduce.9.cloned.1.call-update) | async-done | bytes 7077904 | tf_op jit(solution)/shard_map/psum | solution.py:52
  311.3 5.2 fusion.127
  320.7 15.5 add_convert_fusion.2
  338.2 12.8 gather_fusion
  350.9 4.0 broadcast.603.clone
  354.9 4.0 broadcast.603.clone.1
  358.9 207.5 %while.60 = (s32[]{:T(128)}, f32[20,128,768]{2,1,0:T(8,128)}, bf16[20,128,768]{2,1,0:T(8,128)(2,1)}, f32[20,128,768]{2,1,0:T(8,128)}, bf16[20,128,768]{2,1,0:T(8...) while((s32[]{:T(128)}, f32[20,128,768]{2,1,0:T(8,128)}, ...), condition=%wide.region_17.18_spmd, body=%wide.region_16.17_spmd.sunk | while | flops 314867712 | bytes 4729531 | solution.py:220
  573.3 3.9 broadcast.603
  577.2 544.5 %while.61 = (s32[]{:T(128)}, f32[3,768,768]{2,1,0:T(8,128)}, f32[3,768,768]{1,2,0:T(8,128)}, f32[3,768]{1,0:T(4,128)S(1)}, f32[20,128,768]{2,1,0:T(8,128)}, /*in...) while((s32[]{:T(128)}, f32[3,768,768]{2,1,0:T(8,128)}, ...), condition=%wide.region_23.24_spmd, body=%wide.region_19.23_spmd.sunk | while | flops 613614336 | bytes 32857364 | solution.py:255
  594.2 4.3 fusion.210
  603.9 3.6 add_select_fusion.3
  620.9 4.3 fusion.210
  647.6 4.3 fusion.210
  657.2 3.6 add_select_fusion.3
  674.3 4.3 fusion.210
  683.9 3.6 add_select_fusion.3
  701.0 4.3 fusion.210
  710.6 3.6 add_select_fusion.3
  727.7 4.3 fusion.210
  754.3 4.3 fusion.210
  781.0 4.3 fusion.210
  790.6 3.6 add_select_fusion.3
  807.7 4.3 fusion.210
  834.3 4.3 fusion.210
  843.9 3.6 add_select_fusion.3
  861.0 4.3 fusion.210
  870.6 3.6 add_select_fusion.3
  887.6 4.3 fusion.210
  897.2 3.6 add_select_fusion.3
  914.3 4.3 fusion.210
  940.9 4.3 fusion.210
  967.6 4.3 fusion.210
  977.2 3.6 add_select_fusion.3
  994.3 4.3 fusion.210
  1003.9 3.6 add_select_fusion.3
  1020.9 4.3 fusion.210
  1030.5 3.6 add_select_fusion.3
  1047.6 4.3 fusion.210
  1057.2 3.6 add_select_fusion.3
  1074.3 4.3 fusion.210
  1101.0 4.3 fusion.210
  1121.8 12.7 gather_fusion.3
  1134.5 5.7 convert_element_type.143
  1140.3 12.7 gather_fusion.1
  1153.0 5.4 convert_element_type.145
  1158.5 223.2 %all-reduce.11.cloned.1.call-done = f32[2304,768]{1,0:T(8,128)} async-done(((f32[2304,768]{1,0:T(8,128)}), f32[2304,768]{1,0:T(8,128)}) %all-reduce.11.cloned.1.call-update) | async-done | bytes 7077904 | tf_op jit(solution)/shard_map/psum | solution.py:52
  1381.7 8.2 fusion.128
  1390.4 8.0 fusion.129
  1401.2 51.2 %while.62 = (s32[]{:T(128)}, bf16[3,768,192]{1,2,0:T(8,128)(2,1)S(1)}, bf16[3,768,192]{1,2,0:T(8,128)(2,1)}, bf16[3,768,192]{1,2,0:T(8,128)(2,1)S(1)}, bf16[3,76...) while((s32[]{:T(128)}, ...), condition=%wide.region_29.30_spmd, body=%wide.region_27.29_spmd.sunk | while | flops 1161510144 | bytes 62592184 | solution.py:275
  1463.2 3.6 fusion.95
  1475.5 4.1 reshape.566
  1483.4 4.1 add_add_fusion
  1494.6 23.7 %all-reduce.3 = (f32[2,3,64]{2,1,0:T(4,128)S(1)}, f32[3,768]{1,0:T(4,128)}) all-reduce(f32[2,3,64]{2,1,0:T(4,128)S(1)} %pad_maximum_fusion.1, f32[3,768]{1,0:T(4,128)S(1)} %copy-done.23), channel_id=1, replica_groups=mesh['dp'=8,'tensor'=4] {'dp'}, use_global_device_ids=true, to_apply=%region_40.41 | all-reduce | flops 2688 | bytes 21504 | tf_op jit(solution)/shard_map/psum | solution.py:347
  1527.2 32.2 %reduce-scatter.13.cloned.1.call-done = bf16[96,576]{1,0:T(8,128)(2,1)} async-done(((bf16[768,576]{1,0:T(8,128)(2,1)}), bf16[96,576]{1,0:T(8,128)(2,1)}) %reduce-scatter.13.cloned.1.call-update) | async-done | bytes 110608
  1561.4 478.2 %all-reduce.13.cloned.1.call-done = (f32[2304,768]{1,0:T(8,128)}, f32[2304,768]{1,0:T(8,128)}) async-done(((f32[2304,768]{1,0:T(8,128)}, f32[2304,768]{1,0:T(8,128)}), (f32[2304,768]{1,0:T(8,128)}, f32[2304,768]{1,0:T(8,128)})) %all-reduce.13.cloned.1.call-update) | async-done | bytes 14155792 | tf_op jit(solution)/shard_map/psum | solution.py:52
  2039.7 5.5 multiply_reduce_fusion.4
  2047.4 40.5 %all-reduce.2 = (f32[768]{0:T(1024)}, f32[768]{0:T(1024)}, f32[768]{0:T(1024)}, f32[3,768]{1,0:T(4,128)}, f32[3,768]{1,0:T(4,128)}, /*index=5*/f32[3,768]{1,0:T(4,128)}) all-reduce(f32[768]{0:T(1024)S(1)} %get-tuple-element.415, f32[768]{0:T(1024)S(1)} %get-tuple-element.414, ...), channel_id=1, replica_groups=mesh['dp'=8,'tensor'=4] {'dp','tensor'}, use_global_device_ids=true, to_apply=%region_34.35 | all-reduce | flops 9216 | bytes 73728 | tf_op jit(solution)/shard_map/psum | solution.py:336
  2088.0 15.1 add_convert_fusion
  (594 shorter events, 685.4 us)
Async XLA Ops:
  7.2 48.9 %copy-start = (bf16[192,768]{1,0:T(8,128)(2,1)S(1)}, bf16[192,768]{1,0:T(8,128)(2,1)}, u32[]{:S(2)}) copy-start(bf16[192,768]{1,0:T(8,128)(2,1)} %param.40) | copy-start | bytes 884740
  7.2 5.9 copy-start.35
  7.2 6.0 copy-start.34
  7.2 6.0 copy-start.26
  7.2 304.1 %all-reduce.9.cloned.1.call-start = ((), (), s32[]{:S(2)}) async-start(), calls=%async_computation.4 | async-start | bytes 14155776 | tf_op jit(solution)/shard_map/psum | solution.py:52
  9.9 8.6 copy-start.14
  13.1 5.4 copy-start.18
  13.2 5.3 copy-start.12
  18.5 3.6 copy-start.9
  18.5 3.6 copy-start.30
  22.1 4.7 copy-start.36
  22.2 3.4 copy-start.11
  53.1 1.9 copy-start.21
  53.1 7.0 copy-start.4
  53.1 7.0 copy-start.5
  53.1 7.0 copy-start.6
  55.0 1.0 copy-start.8
  56.0 4.2 copy-start.20
  60.1 1321.6 %all-reduce.11.cloned.1.call-start = ((), (), s32[]{:S(2)}) async-start(), calls=%async_computation.5 | async-start | bytes 14155776 | tf_op jit(solution)/shard_map/psum | solution.py:52
  75.1 13.2 copy-start.31
  75.1 13.2 copy-start.32
  75.1 236.2 %copy-start.24 = (f32[768]{0:T(1024)S(1)}, f32[768]{0:T(1024)}, u32[]{:S(2)}) copy-start(f32[768]{0:T(1024)} %param.41) | copy-start | bytes 9220
  88.4 0.6 copy-start.16
  311.3 5.2 copy-start.1
  311.3 7.1 copy-start.2
  569.8 7.4 copy-start.28
  569.8 7.4 copy-start.29
  1121.7 12.7 copy-start.22
  1134.5 355.5 %reduce-scatter.9.cloned.1.call-start = ((), (), s32[]{:S(2)}) async-start(), calls=%async_computation.6 | async-start | bytes 3981312 | tf_op jit(solution)/shard_map/reduce_scatter | solution.py:329
  1140.2 351.7 %reduce-scatter.11.cloned.1.call-start = ((), (), s32[]{:S(2)}) async-start(), calls=%async_computation.7 | async-start | bytes 3981312 | tf_op jit(solution)/shard_map/reduce_scatter | solution.py:332
  1153.0 236.9 %slice-start = ((s8[7077888]{0:T(1024)(128)(4,1)}), s8[2883584]{0:T(1024)(128)(4,1)S(1)}, s32[]{:S(2)}) async-start(s8[7077888]{0:T(1024)(128)(4,1)} %bitcast.359), calls=%async_computation.11 | async-start | bytes 5767168
  1158.4 367.2 %reduce-scatter.15.cloned.1.call-start = ((), (), s32[]{:S(2)}) async-start(), calls=%async_computation.9 | async-start | bytes 442368
  1381.7 8.3 slice-start.1
  1381.7 8.7 copy-start.3
  1398.4 1.8 copy-start.7
  1398.4 2.8 copy-start.37
  1466.8 92.5 %reduce-scatter.13.cloned.1.call-start = ((), (), s32[]{:S(2)}) async-start(), calls=%async_computation.8 | async-start | bytes 1105920
  1479.6 560.0 %all-reduce.13.cloned.1.call-start = ((), (), s32[]{:S(2)}) async-start(), calls=%async_computation.10 | async-start | bytes 28311552 | tf_op jit(solution)/shard_map/psum | solution.py:52
  1479.7 2.5 copy-start.13
  1482.2 1.2 copy-start.10
  1487.5 0.8 copy-start.17
  1487.5 2.4 copy-start.33
  1487.5 7.1 copy-start.23
  1487.5 552.2 %copy-start.15 = (f32[2304]{0:T(1024)S(1)}, f32[2304]{0:T(1024)}, u32[]{:S(2)}) copy-start(f32[2304]{0:T(1024)} %copy-done.14) | copy-start | bytes 27652
  1487.5 552.2 %copy-start.19 = (f32[2304]{0:T(1024)S(1)}, f32[2304]{0:T(1024)}, u32[]{:S(2)}) copy-start(f32[2304]{0:T(1024)} %copy-done.18) | copy-start | bytes 27652
  1487.5 552.1 %copy-start.27 = (f32[768]{0:T(1024)S(1)}, f32[768]{0:T(1024)}, u32[]{:S(2)}) copy-start(f32[768]{0:T(1024)} %param.36) | copy-start | bytes 9220
  2039.7 48.3 %copy-start.25 = (f32[768]{0:T(1024)S(1)}, f32[768]{0:T(1024)}, u32[]{:S(2)}) copy-start(f32[768]{0:T(1024)} %param.41) | copy-start | bytes 9220
Sparse Core Ops, SparseCore 0:
  60.2 251.0 all-reduce.8
  1134.6 247.0 all-reduce.10
  1385.2 46.9 reduce-scatter.8
  1435.6 48.0 reduce-scatter.10
  1486.6 33.8 reduce-scatter.14
  1523.5 35.7 reduce-scatter.12
  1562.1 477.5 all-reduce.12
where the time goes:
time: 2130 us; the launch traced here: 2110 us
  waiting for transfers between devices  956 us (45%)
  matrix products  450 us (21%)
  local copies, waits for them, and re-layouts  346 us (16%)
  other arithmetic  184 us (9%)
  loops' own time  94.3 us (4%)
  blocking collectives  64.2 us (3%)
    psum x3, waiting for transfers between devices, total_rows(): return lax.psum(values, 'tensor')  924 us
    another operation x50, local copies, waits for them, and re-layouts  126 us
    dot_general x20, matrix products, expert_back(): jnp.einsum('rd,rf->df', block_in, grad_pre, preferred_element_type=jnp.fl...  86.6 us
    scatter-add x40, local copies, waits for them, and re-layouts, expert_back(): acc_down.at[expert_id]  72.3 us
    dot_general x20, matrix products, expert_back(): jnp.einsum('rf,rd->fd', act_out, grad_block, preferred_element_type=jnp.f...  71.4 us
    dot_general x20, matrix products, expert_block(): block_out = jnp.dot(act_out, down_mat, preferred_element_type=jnp.float32)  62.2 us
    dot_general x20, matrix products, expert_back(): jnp.einsum('rd,fd->rf', grad_block, down_mat, preferred_element_type=jnp....  52.5 us
    dot_general x20, matrix products, expert_back(): jnp.einsum('rf,df->rd', grad_pre, up_mat, preferred_element_type=jnp.floa...  51.5 us
  transfers between devices with their start and end apart: 7, of which 4 were waited for; matrix products, arithmetic and copies ran while one was open for 8% of the time, Pallas kernels for 0%

commit v1 on v0

v1 whole, which is shorter than its diff:
```python
import math

import jax
import jax.numpy as jnp
from jax import lax
from jax.experimental import pallas as pl
from jax.experimental.pallas import tpu as pltpu
from jax.sharding import PartitionSpec as P

HEAD_DIM = 64
S = 768
TILE = 192
BACK = 672
EPS = 1e-05
MASKED = -1000000000.0
SCALE = 1.0 / math.sqrt(HEAD_DIM)
F32 = jnp.float32
BF16 = jnp.bfloat16

NN = (((1,), (0,)), ((), ()))
NT = (((1,), (1,)), ((), ()))
TN = (((0,), (0,)), ((), ()))


def mm(a, b, dims=NN):
    return lax.dot_general(a, b, dims, preferred_element_type=F32)


def layer_norm(values):
    centred = values - jnp.mean(values, -1, keepdims=True)
    rstd = lax.rsqrt(jnp.mean(centred * centred, -1, keepdims=True) + EPS)
    return centred * rstd, rstd


def norm_back(scaled, xhat, rstd):
    return rstd * (
        scaled
        - jnp.mean(scaled, -1, keepdims=True)
        - xhat * jnp.mean(scaled * xhat, -1, keepdims=True)
    )


def pick_rows(table_ref, expert):
    out = jnp.where(expert == 0, table_ref[0:1, :], table_ref[1:2, :])
    return jnp.where(expert == 2, table_ref[2:3, :], out)


def cost(flops, nbytes, trans=0):
    return pl.CostEstimate(flops=int(flops), bytes_accessed=int(nbytes), transcendentals=int(trans))


def params(**kw):
    return pltpu.CompilerParams(vmem_limit_bytes=56 * 1024 * 1024, **kw)


def attn_fwd_kernel(x_ref, g_ref, b_ref, wt_ref, wb_ref, kb_ref, n1_ref, qkv_ref, mix_ref, lse_ref):
    width = wt_ref.shape[0] // 3
    heads = width // HEAD_DIM
    xhat, _ = layer_norm(x_ref[...].astype(F32))
    normed = (xhat * g_ref[...] + b_ref[...]).astype(BF16)
    n1_ref[...] = normed
    for j in range(3):
        rows = pl.ds(j * width, width)
        part = (mm(wt_ref[rows, :], normed, NT) + wb_ref[rows, :]).astype(BF16)
        if j == 0:
            part = part * jnp.asarray(SCALE, BF16)
        qkv_ref[rows, :] = part
    half = S // 2
    for h in range(heads):
        kt = qkv_ref[pl.ds(width + h * HEAD_DIM, HEAD_DIM), :]
        vt = qkv_ref[pl.ds(2 * width + h * HEAD_DIM, HEAD_DIM), :]
        k = kt.T
        for c in range(2):
            cols = pl.ds(c * half, half)
            qt = qkv_ref[pl.ds(h * HEAD_DIM, HEAD_DIM), cols]
            s = mm(k, qt) + kb_ref[:, c : c + 1]
            top = jnp.max(s, 0, keepdims=True)
            p = jnp.exp(s - top)
            total = jnp.sum(p, 0, keepdims=True)
            o = mm(vt, p.astype(BF16)) * (1.0 / total)
            mix_ref[pl.ds(h * HEAD_DIM, HEAD_DIM), cols] = o.astype(BF16)
            lse_ref[pl.ds(h, 1), cols] = top + jnp.log(total)


def attn_fwd(x, g, b, wt, wb, kb):
    rows, model = x.shape
    width = wt.shape[0] // 3
    heads = width // HEAD_DIM
    return pl.pallas_call(
        attn_fwd_kernel,
        out_shape=(
            jax.ShapeDtypeStruct((rows, model), BF16),
            jax.ShapeDtypeStruct((3 * width, rows), BF16),
            jax.ShapeDtypeStruct((width, rows), BF16),
            jax.ShapeDtypeStruct((heads, rows), F32),
        ),
        compiler_params=params(),
        cost_estimate=cost(2 * rows * model * 3 * width + heads * 8 * rows * rows * 256, 8e6, heads * rows * rows),
        name="attn_fwd",
    )(x, g, b, wt, wb, kb)


def expert_kernel(
    flags_ref, own_ref, pair_ref, far_a_ref, far_b_ref, wo_ref, x_ref, cot_ref, eid_ref,
    ob_ref, g2_ref, b2_ref, ub_ref, up_ref, down_ref,
    mid_ref, n2_ref, act_ref, gpre_ref, out_ref, gn2_ref, small_ref,
    up_v, down_v, xhat_v, gn2_v, sems,
):
    width = own_ref.shape[0]
    experts = up_ref.shape[0]
    up_copy = pltpu.make_async_copy(up_ref, up_v, sems.at[0])
    down_copy = pltpu.make_async_copy(down_ref, down_v, sems.at[1])
    up_copy.start()
    down_copy.start()
    expert = eid_ref[...]
    proj = mm(own_ref[...], wo_ref[0:width, :], TN)
    proj += mm(pair_ref[...], wo_ref[width : 2 * width, :], TN)
    proj += mm(far_a_ref[...] + far_b_ref[...], wo_ref[2 * width :, :], TN)
    middle = x_ref[...].astype(F32) + (proj + ob_ref[...])
    mid_ref[...] = middle
    xhat, _ = layer_norm(middle)
    xhat_v[...] = xhat
    n2_ref[...] = (xhat * pick_rows(g2_ref, expert) + pick_rows(b2_ref, expert)).astype(BF16)
    act_ref[...] = jnp.zeros_like(act_ref)
    gpre_ref[...] = jnp.zeros_like(gpre_ref)
    out_ref[...] = jnp.zeros_like(out_ref)
    gn2_v[...] = jnp.zeros_like(gn2_v)
    small_ref[...] = jnp.zeros_like(small_ref)
    up_copy.wait()
    down_copy.wait()

    def step(i, carry):
        tile, e = i // experts, lax.rem(i, experts)

        @pl.when(flags_ref[i] > 0)
        def _():
            rows = pl.ds(pl.multiple_of(tile * TILE, TILE), TILE)
            mask = (eid_ref[rows, :] == e).astype(F32)
            cot = cot_ref[rows, :]
            pre = mm(n2_ref[rows, :], up_v[e]) + ub_ref[pl.ds(e, 1), :]
            cdf = 0.5 + 0.5 * lax.erf(pre * (1.0 / math.sqrt(2.0)))
            act = (pre * cdf * mask).astype(BF16)
            slope = cdf + pre * (jnp.exp(-0.5 * pre * pre) * (1.0 / math.sqrt(2.0 * math.pi)))
            gpre = (mm(cot, down_v[e], NT) * slope * mask).astype(BF16)
            gn2 = mm(gpre, up_v[e], NT)
            out = mm(act, down_v[e])
            act_ref[rows, :] = act_ref[rows, :] + act
            gpre_ref[rows, :] = gpre_ref[rows, :] + gpre
            out_ref[rows, :] = out_ref[rows, :] + out.astype(BF16)
            gn2_v[rows, :] = gn2_v[rows, :] + gn2.astype(BF16)
            for j, values in enumerate(
                (gn2 * xhat_v[rows, :], gn2, gpre.astype(F32), cot.astype(F32) * mask)
            ):
                at = pl.ds(j * experts + e, 1)
                small_ref[at, :] = small_ref[at, :] + jnp.sum(values, 0, keepdims=True)

        return carry

    lax.fori_loop(0, (S // TILE) * experts, step, 0)
    gn2_ref[...] = gn2_v[0:BACK, :]


def expert_fwd_bwd(flags, own, pair, far_a, far_b, wo, x, cot, eid, ob, g2, b2, ub, up, down):
    rows, model = x.shape
    experts, _, hidden = up.shape
    vmem = pl.BlockSpec(memory_space=pltpu.VMEM)
    hbm = pl.BlockSpec(memory_space=pl.ANY)
    return pl.pallas_call(
        expert_kernel,
        out_shape=(
            jax.ShapeDtypeStruct((rows, model), F32),
            jax.ShapeDtypeStruct((rows, model), BF16),
            jax.ShapeDtypeStruct((rows, hidden), BF16),
            jax.ShapeDtypeStruct((rows, hidden), BF16),
            jax.ShapeDtypeStruct((rows, model), BF16),
            jax.ShapeDtypeStruct((BACK, model), BF16),
            jax.ShapeDtypeStruct((4 * experts, model), F32),
        ),
        in_specs=[pl.BlockSpec(memory_space=pltpu.SMEM)] + [vmem] * 12 + [hbm] * 2,
        out_specs=(vmem,) * 7,
        scratch_shapes=[
            pltpu.VMEM(up.shape, BF16),
            pltpu.VMEM(down.shape, BF16),
            pltpu.VMEM((rows, model), F32),
            pltpu.VMEM((rows, model), BF16),
            pltpu.SemaphoreType.DMA((2,)),
        ],
        compiler_params=params(),
        cost_estimate=cost(2 * rows * model * model + 1.6 * 8 * rows * model * hidden, 22e6, 2 * rows * hidden),
        name="expert_fwd_bwd",
    )(flags, own, pair, far_a, far_b, wo, x, cot, eid, ob, g2, b2, ub, up, down)


def expert_grads_kernel(flags_ref, *refs):
    windows = (len(refs) - 2) // 5
    groups = [refs[5 * w : 5 * w + 5] for w in range(windows)]
    out_ref, acc = refs[-2:]
    experts = pl.num_programs(0)
    e = pl.program_id(0)
    tiles = S // TILE
    model = out_ref.shape[0]
    acc[...] = jnp.zeros_like(acc)
    for w, (n2_ref, act_ref, gpre_ref, cot_ref, eid_ref) in enumerate(groups):

        def step(tile, carry):
            @pl.when(flags_ref[(w * tiles + tile) * experts + e] > 0)
            def _():
                rows = pl.ds(pl.multiple_of(tile * TILE, TILE), TILE)
                mask = (eid_ref[rows, :] == e).astype(BF16)
                acc[:, 0:model] += mm(n2_ref[rows, :], gpre_ref[rows, :] * mask, TN)
                acc[:, model:] += mm(cot_ref[rows, :], act_ref[rows, :] * mask, TN)

            return carry

        lax.fori_loop(0, tiles, step, 0)
    out_ref[...] = acc[...].astype(BF16)


def expert_grads(flags, groups, experts):
    rows, model = groups[0][0].shape
    hidden = groups[0][1].shape[1]
    flat = [a for g in groups for a in g]
    whole = lambda a: pl.BlockSpec(a.shape, lambda e: (0, 0), pipeline_mode=pl.Buffered(1))
    return pl.pallas_call(
        expert_grads_kernel,
        grid=(experts,),
        out_shape=jax.ShapeDtypeStruct((model, experts * 2 * hidden), BF16),
        in_specs=[pl.BlockSpec(memory_space=pltpu.SMEM)] + [whole(a) for a in flat],
        out_specs=pl.BlockSpec((model, 2 * hidden), lambda e: (0, e)),
        scratch_shapes=[pltpu.VMEM((model, 2 * hidden), F32)],
        compiler_params=params(),
        cost_estimate=cost(1.5 * 4 * len(groups) * rows * model * hidden, 22e6),
        name="expert_grads",
    )(flags, *flat)


def mid_back_kernel(s_ref, r_ref, mid_ref, cot_ref, eid_ref, g2_ref, gm_ref, ga_ref):
    total = s_ref[...].astype(F32) + r_ref[...].astype(F32)
    xhat, rstd = layer_norm(mid_ref[...])
    grad = cot_ref[...].astype(F32) + norm_back(total * pick_rows(g2_ref, eid_ref[...]), xhat, rstd)
    gm_ref[...] = grad
    ga_ref[...] = grad.astype(BF16)


def mid_back(s, r, mid, cot, eid, g2):
    model = s.shape[1]
    block = BACK // 3
    row = lambda n: pl.BlockSpec((block, n), lambda i: (i, 0))
    return pl.pallas_call(
        mid_back_kernel,
        grid=(3,),
        out_shape=(jax.ShapeDtypeStruct(s.shape, F32), jax.ShapeDtypeStruct(s.shape, BF16)),
        in_specs=[row(model)] * 4 + [row(1), pl.BlockSpec(g2.shape, lambda i: (0, 0))],
        out_specs=(row(model), row(model)),
        compiler_params=params(),
        cost_estimate=cost(30 * s.size, 16 * s.size),
        name="mid_back",
    )(s, r, mid, cot, eid, g2)


def attn_bwd_kernel(
    flag_ref, ga_ref, far_ref, wo_ref, qkv_ref, mix_ref, lse_ref, kb_ref, wt_ref,
    gaf_ref, dqkv_ref, gn1_ref, gmt_v,
):
    width = wo_ref.shape[0]
    heads = width // HEAD_DIM
    take = flag_ref[0] > 0

    @pl.when(take)
    def _():
        gaf_ref[0:BACK, :] = far_ref[...]

    @pl.when(jnp.logical_not(take))
    def _():
        gaf_ref[0:BACK, :] = ga_ref[...]

    gaf_ref[BACK:, :] = jnp.zeros((S - BACK, gaf_ref.shape[1]), BF16)
    gmt_v[...] = mm(wo_ref[...], gaf_ref[...], NT).astype(BF16)
    half = S // 2
    for h in range(heads):
        at = pl.ds(h * HEAD_DIM, HEAD_DIM)
        kt = qkv_ref[pl.ds(width + h * HEAD_DIM, HEAD_DIM), :]
        vt = qkv_ref[pl.ds(2 * width + h * HEAD_DIM, HEAD_DIM), :]
        k, v = kt.T, vt.T
        dk = dv = None
        for c in range(2):
            cols = pl.ds(c * half, half)
            qt = qkv_ref[at, cols]
            dot = gmt_v[at, cols]
            delta = jnp.sum(dot.astype(F32) * mix_ref[at, cols].astype(F32), 0, keepdims=True)
            s = mm(k, qt) + kb_ref[:, c : c + 1]
            p = jnp.exp(s - lse_ref[pl.ds(h, 1), cols])
            ds = (p * (mm(v, dot) - delta)).astype(BF16)
            dv_c = mm(p.astype(BF16), dot, NT)
            dk_c = mm(ds, qt, NT)
            dv = dv_c if dv is None else dv + dv_c
            dk = dk_c if dk is None else dk + dk_c
            dqkv_ref[at, cols] = (mm(kt, ds) * SCALE).astype(BF16)
        dqkv_ref[pl.ds(width + h * HEAD_DIM, HEAD_DIM), :] = dk.astype(BF16).T
        dqkv_ref[pl.ds(2 * width + h * HEAD_DIM, HEAD_DIM), :] = dv.astype(BF16).T
    gn1_ref[...] = mm(dqkv_ref[:, 0:BACK], wt_ref[...], TN).astype(BF16)


def attn_bwd(flag, ga, far, wo, qkv, mix, lse, kb, wt):
    width, model = wo.shape
    rows = qkv.shape[1]
    heads = width // HEAD_DIM
    vmem = pl.BlockSpec(memory_space=pltpu.VMEM)
    return pl.pallas_call(
        attn_bwd_kernel,
        out_shape=(
            jax.ShapeDtypeStruct((rows, model), BF16),
            jax.ShapeDtypeStruct(qkv.shape, BF16),
            jax.ShapeDtypeStruct((BACK, model), BF16),
        ),
        in_specs=[pl.BlockSpec(memory_space=pltpu.SMEM)] + [vmem] * 8,
        out_specs=(vmem,) * 3,
        scratch_shapes=[pltpu.VMEM((width, rows), BF16)],
        compiler_params=params(),
        cost_estimate=cost(2 * rows * model * 4 * width + heads * 16 * rows * rows * 256, 9e6, heads * rows * rows),
        name="attn_bwd",
    )(flag, ga, far, wo, qkv, mix, lse, kb, wt)


def attn_grads_kernel(*refs):
    windows = (len(refs) - 4) // 6
    groups = [refs[6 * w : 6 * w + 6] for w in range(windows)]
    out_ref, rows_ref, cols_ref, acc = refs[-4:]
    wide = groups[0][1].shape[0]
    rows_ref[...] = jnp.zeros_like(rows_ref)
    cols = None
    for w, (n1_ref, dqkv_ref, mix_ref, gaf_ref, x_ref, gn1_ref) in enumerate(groups):
        qkv_part = mm(dqkv_ref[...], n1_ref[...])
        out_part = mm(mix_ref[...], gaf_ref[...])
        if w == 0:
            acc[0:wide, :] = qkv_part
            acc[wide:, :] = out_part
        else:
            acc[0:wide, :] += qkv_part
            acc[wide:, :] += out_part
        col = jnp.sum(dqkv_ref[...].astype(F32), 1, keepdims=True)
        cols = col if cols is None else cols + col
        xhat, _ = layer_norm(x_ref[0:BACK, :].astype(F32))
        grad = gn1_ref[...].astype(F32)
        for j, values in enumerate((grad * xhat, grad, gaf_ref[...].astype(F32))):
            rows_ref[j : j + 1, :] = rows_ref[j : j + 1, :] + jnp.sum(values, 0, keepdims=True)
    cols_ref[...] = cols
    out_ref[...] = acc[...].astype(BF16).T


def attn_grads(groups):
    n1, dqkv, mix = groups[0][:3]
    wide = dqkv.shape[0] + mix.shape[0]
    model = n1.shape[1]
    flat = [a for g in groups for a in g]
    return pl.pallas_call(
        attn_grads_kernel,
        out_shape=(
            jax.ShapeDtypeStruct((model, wide), BF16),
            jax.ShapeDtypeStruct((8, model), F32),
            jax.ShapeDtypeStruct((dqkv.shape[0], 1), F32),
        ),
        scratch_shapes=[pltpu.VMEM((wide, model), F32)],
        compiler_params=params(),
        cost_estimate=cost(len(groups) * 2 * n1.shape[0] * model * wide, 18e6),
        name="attn_grads",
    )(*flat)


def first_back_kernel(s_ref, r_ref, gm_ref, x_ref, g_ref, out_ref):
    total = s_ref[...].astype(F32) + r_ref[...].astype(F32)
    xhat, rstd = layer_norm(x_ref[...].astype(F32))
    out_ref[...] = (gm_ref[...] + norm_back(total * g_ref[...], xhat, rstd)).astype(BF16)


def first_back(s, r, gm, x, g):
    model = s.shape[1]
    block = BACK // 3
    row = lambda n: pl.BlockSpec((block, n), lambda i: (i, 0))
    return pl.pallas_call(
        first_back_kernel,
        grid=(3,),
        out_shape=jax.ShapeDtypeStruct(s.shape, BF16),
        in_specs=[row(model)] * 4 + [pl.BlockSpec(g.shape, lambda i: (0, 0))],
        out_specs=row(model),
        compiler_params=params(),
        cost_estimate=cost(30 * s.size, 12 * s.size),
        name="first_back",
    )(s, r, gm, x, g)


def layer_out_kernel(s_ref, r_ref, mid_ref, eid_ref, db_ref, out_ref):
    total = s_ref[...].astype(F32) + r_ref[...].astype(F32)
    out_ref[...] = (mid_ref[...] + (total + pick_rows(db_ref, eid_ref[...]))).astype(BF16)


def layer_out_rows(s, r, mid, eid, db):
    rows, model = s.shape
    row = lambda n: pl.BlockSpec((TILE, n), lambda i: (i, 0))
    return pl.pallas_call(
        layer_out_kernel,
        grid=(rows // TILE,),
        out_shape=jax.ShapeDtypeStruct(s.shape, BF16),
        in_specs=[row(model)] * 3 + [row(1), pl.BlockSpec(db.shape, lambda i: (0, 0))],
        out_specs=row(model),
        compiler_params=params(),
        cost_estimate=cost(5 * s.size, 10 * s.size),
        name="layer_out_rows",
    )(s, r, mid, eid, db)


def inward(v):
    return lax.ppermute(v, "tensor", [(0, 1), (3, 2)])


def across(v):
    return lax.ppermute(v, "tensor", [(1, 2), (2, 1)])


def outward(v):
    return lax.ppermute(v, "tensor", [(1, 0), (2, 3)])


def pairs(v):
    return lax.ppermute(v, "tensor", [(0, 1), (1, 0), (2, 3), (3, 2)])


def add_rounded(a, b):
    return (a.astype(F32) + b.astype(F32)).astype(BF16)


def body(
    inputs, cotangent, row_expert, row_keep, window_resolution, attention_norm_gain,
    attention_norm_bias, qkv_weight, qv_bias, out_weight, out_bias, second_gain,
    expert_norm_bias, up_weight, up_bias, down_weight, down_bias,
):
    row_count, model = inputs.shape
    experts = up_weight.shape[0]
    width = qkv_weight.shape[2]
    windows = row_count // S
    tiles = S // TILE
    me = lax.axis_index("tensor")
    at_end = (me == 0) | (me == 3)
    end_flag = at_end.astype(jnp.int32).reshape(1)

    wt = jnp.transpose(qkv_weight, (0, 2, 1)).reshape(3 * width, model)
    bias_pair = qv_bias.reshape(2, width)
    wb = jnp.concatenate([bias_pair[0], jnp.zeros((width,), F32), bias_pair[1]]).reshape(3 * width, 1)
    keep = row_keep.reshape(windows, S) > 0
    single = window_resolution.reshape(windows, 1) > 0
    upper = (jnp.arange(S) >= S // 2)[None, :]
    kb = jnp.stack([keep & (single | ~upper), keep & (single | upper)], -1)
    kb = jnp.where(kb, 0.0, MASKED).astype(F32)
    eid = row_expert.reshape(windows, S, 1)
    onehot = row_expert.reshape(windows, tiles, TILE, 1) == jnp.arange(experts)
    flags = jnp.any(onehot, 2).astype(jnp.int32).reshape(windows, tiles * experts)
    real = onehot & (row_keep.reshape(windows, tiles, TILE, 1) > 0)
    back_flags = jnp.any(real, 2).astype(jnp.int32).reshape(-1)
    g1, b1 = attention_norm_gain.reshape(1, model), attention_norm_bias.reshape(1, model)
    ob = out_bias.reshape(1, model)

    shards = lax.all_gather(out_weight, "tensor", axis=0)
    near = me ^ 1
    far = jnp.where(me < 2, 2, 1)
    order = jnp.stack([me, near, far, jnp.where(me < 2, 3, 0)])
    wo_all = shards[order].reshape(model, model)

    xs = [inputs[w * S : (w + 1) * S] for w in range(windows)]
    cots = [cotangent[w * S : (w + 1) * S] for w in range(windows)]

    fwd = [attn_fwd(xs[w], g1, b1, wt, wb, kb[w]) for w in range(windows)]
    ex = []
    for w in range(windows):
        own = fwd[w][2]
        pair = pairs(own)
        far_a = across(jnp.concatenate([own, pair], 0))
        far_b = outward(far_a)
        ex.append(
            expert_fwd_bwd(
                flags[w], own, pair, far_a, far_b, wo_all, xs[w], cots[w], eid[w],
                ob, second_gain, expert_norm_bias, up_bias, up_weight, down_weight,
            )
        )
    mids = []
    for w in range(windows):
        mid, gn2 = ex[w][0], ex[w][5]
        s = add_rounded(gn2, inward(gn2))
        mids.append(mid_back(s, across(s), mid[:BACK], cots[w][:BACK], eid[w][:BACK], second_gain))
    bwd = []
    for w in range(windows):
        n1, qkv, mix, lse = fwd[w]
        ga = mids[w][1]
        bwd.append(attn_bwd(end_flag, ga, outward(ga), out_weight, qkv, mix, lse, kb[w], wt))
    rows_grad = []
    for w in range(windows):
        gn1 = bwd[w][2]
        s = add_rounded(gn1, inward(gn1))
        grad = first_back(s, across(s), mids[w][0], xs[w][:BACK], g1)
        grad = jnp.where(at_end, outward(grad), grad)
        rows_grad.append(jnp.concatenate([grad, jnp.zeros((S - BACK, model), BF16)], 0))
    outs = []
    for w in range(windows):
        part = ex[w][4]
        s = add_rounded(part, inward(part))
        rows_out = layer_out_rows(s, across(s), ex[w][0], eid[w], down_bias)
        outs.append(jnp.where(at_end, outward(rows_out), rows_out))

    groups = [(ex[w][1], ex[w][2], ex[w][3], cots[w], eid[w]) for w in range(windows)]
    expert_g = expert_grads(back_flags, groups, experts)
    expert_g = lax.psum_scatter(expert_g, "dp", scatter_dimension=0, tiled=True).astype(F32)
    groups = [(fwd[w][0], bwd[w][1], fwd[w][2], bwd[w][0], xs[w], bwd[w][2]) for w in range(windows)]
    attn_g, row_sums, col_sums = attn_grads(groups)
    attn_g = lax.psum_scatter(attn_g, "dp", scatter_dimension=0, tiled=True).astype(F32)

    shared = jnp.where(me == 0, 1.0, 0.0)
    small = sum(ex[w][6] for w in range(windows))
    whole = jnp.concatenate(
        [
            small[: 2 * experts],
            small[3 * experts :] * shared,
            row_sums[0:2],
            row_sums[2:3] * shared,
        ],
        0,
    )
    whole = lax.psum(whole, ("dp", "tensor"))
    local = lax.psum(
        jnp.concatenate([small[2 * experts : 3 * experts].reshape(-1), col_sums.reshape(-1)]), "dp"
    )
    block = expert_g.shape[0]
    hidden = up_weight.shape[2]
    expert_g = expert_g.reshape(block, experts, 2, hidden)
    grad_up = jnp.transpose(expert_g[:, :, 0], (1, 0, 2))
    grad_down = jnp.transpose(expert_g[:, :, 1], (1, 2, 0))
    grad_qkv = jnp.transpose(attn_g[:, : 3 * width].reshape(block, 3, width), (1, 0, 2))
    grad_out = attn_g[:, 3 * width :].T
    up_bias_grad = local[: experts * hidden].reshape(experts, hidden)
    cols = local[experts * hidden :].reshape(3, width)
    qv_grad = jnp.stack([cols[0], cols[2]]).reshape(qv_bias.shape)
    return (
        jnp.concatenate(outs, 0),
        jnp.concatenate(rows_grad, 0),
        whole[3 * experts],
        whole[3 * experts + 1],
        grad_qkv,
        qv_grad,
        grad_out,
        whole[3 * experts + 2],
        whole[:experts],
        whole[experts : 2 * experts],
        grad_up,
        up_bias_grad,
        grad_down,
        whole[2 * experts : 3 * experts],
    )


def solution(mesh):
    in_specs = (
        P("dp", None), P("dp", None), P("dp"), P("dp"), P("dp"), P(), P(),
        P(None, None, "tensor"), P(None, "tensor", None), P("tensor", None), P(), P(), P(),
        P(None, None, "tensor"), P(None, "tensor"), P(None, "tensor", None), P(),
    )
    out_specs = (
        P("dp", None), P("dp", None), P(), P(), P(None, "dp", "tensor"), P(None, "tensor", None),
        P("tensor", "dp"), P(), P(), P(), P(None, "dp", "tensor"), P(None, "tensor"),
        P(None, "tensor", "dp"), P(),
    )
    return jax.shard_map(body, mesh=mesh, in_specs=in_specs, out_specs=out_specs, check_vma=False)
```

time: 2130 us -> 629 us (0.30)
  waiting for transfers between devices: 956 us -> 196 us
  matrix products: 450 us -> 0 us
  local copies, waits for them, and re-layouts: 346 us -> 56.9 us
  Pallas kernels: 0 us -> 181 us
  other arithmetic: 184 us -> 29.2 us
  loops' own time: 94.3 us -> 0 us
  starting transfers between devices: 0.29 us -> 86.3 us
    psum x3 -> x0, waiting for transfers between devices: 924 us -> none  [total_rows(): return lax.psum(values, 'tensor')]
    dot_general x156 -> x0, matrix products: 450 us -> none  [the longest x20 86.6 us: expert_back(): jnp.einsum('rd,rf->df', block_in, grad_pre, preferred_element_type=jnp.fl...]
    ppermute x0 -> x36, waiting for transfers between devices: none -> 196 us  [the longest x9 91 us: inward(): return lax.ppermute(v, 'tensor', [(0, 1), (3, 2)])]
    pallas_call x0 -> x20, Pallas kernels: none -> 181 us  [the longest x3 48.9 us: expert_fwd_bwd(): pl.pallas_call(expert_kernel, out_shape=(jax.ShapeDtypeStruct((rows, mode...]
    another operation x52 -> x3, local copies, waits for them, and re-layouts: 126 us -> 0.69 us  [the longest x1 0.52 us: body(): kb = jnp.stack([keep & (single | ~upper), keep & (single | upper)], -1)]
    another operation x4 -> x0, loops' own time: 94.3 us -> none  [the longest x1 50.8 us: body(): lax.scan(expert_back, start_state, (hidden_in, pre_blocks, act_blocks, gr...]
    ppermute x0 -> x36, starting transfers between devices: none -> 85.4 us  [the longest x9 47.6 us: inward(): return lax.ppermute(v, 'tensor', [(0, 1), (3, 2)])]
    scatter-add x60 -> x0, local copies, waits for them, and re-layouts: 73.5 us -> none  [the longest x40 72.3 us: expert_back(): acc_down.at[expert_id]]
  transfers between devices with their start and end apart: 7 -> 39, of which waited for: 4 -> 14; matrix products, arithmetic and copies ran while one was open for 8% -> 11% of each run, Pallas kernels for 0% -> 24%
where the time goes in v1:
time: 629 us; the launch traced here: 624 us
  waiting for transfers between devices  196 us (31%)
  Pallas kernels  181 us (29%)
  starting transfers between devices  86.3 us (14%)
  blocking collectives  59.7 us (9%)
  local copies, waits for them, and re-layouts  56.9 us (9%)
  other arithmetic  29.2 us (5%)
  between operations  14.8 us (2%)
    ppermute x9, waiting for transfers between devices, inward(): return lax.ppermute(v, 'tensor', [(0, 1), (3, 2)])  91 us
    ppermute x12, waiting for transfers between devices, outward(): return lax.ppermute(v, 'tensor', [(1, 0), (2, 3)])  87.3 us
    pallas_call x3, Pallas kernels, expert_fwd_bwd(): pl.pallas_call(expert_kernel, out_shape=(jax.ShapeDtypeStruct((rows, mode...  48.9 us
    ppermute x9, starting transfers between devices, inward(): return lax.ppermute(v, 'tensor', [(0, 1), (3, 2)])  47.6 us
    psum x1, blocking collectives, body(): whole = lax.psum(whole, ('dp', 'tensor'))  37.4 us
    pallas_call x3, Pallas kernels, attn_bwd(): pl.pallas_call(attn_bwd_kernel, out_shape=(jax.ShapeDtypeStruct((rows, mo...  30.5 us
    psum x1, blocking collectives, body(): lax.psum(jnp.concatenate([small[2 * experts:3 * experts].reshape(-1), col...  22.3 us
    pallas_call x3, Pallas kernels, attn_fwd(): pl.pallas_call(attn_fwd_kernel, out_shape=(jax.ShapeDtypeStruct((rows, mo...  21.6 us
  transfers between devices with their start and end apart: 39, of which 14 were waited for; matrix products, arithmetic and copies ran while one was open for 11% of the time, Pallas kernels for 24%

profile of v1, /device:TPU:0, one launch (start us, length us, event | category | flops | bytes accessed | tf_op | source)
XLA Modules:
  0.0 623.6 jit_solution(1900306729991165353)
XLA Ops:
  11.7 1.9 fusion.8
  15.3 7.2 %attn_fwd.3 = (bf16[768,768]{1,0:T(8,128)(2,1)}, bf16[576,768]{1,0:T(8,128)(2,1)}, bf16[192,768]{1,0:T(8,128)(2,1)}, f32[3,768]{1,0:T(4,128)}) custom-call(bf16[768,768]{1,0:T(8,128)(2,1)} %get-tuple-element.188.x_ref.refs_4_, f32[1,768]{1,0:T(1,128)} %reshape.407.g_ref, f32[1,768]{1,0:T(1,128)} %reshape.408.b_ref, bf16[576,768]{1,0:T(8,128)(2,1)} %bitcast.42, ...), custom_call_target="tpu_custom_call" | custom-call | flops 4303355904 | bytes 8000000 | tf_op jit(solution)/shard_map/attn_fwd/pallas_call | solution.py:89
  22.5 3.0 collective-permute-start
  26.1 7.2 %attn_fwd.5 = (bf16[768,768]{1,0:T(8,128)(2,1)}, bf16[576,768]{1,0:T(8,128)(2,1)}, bf16[192,768]{1,0:T(8,128)(2,1)}, f32[3,768]{1,0:T(4,128)}) custom-call(bf16[768,768]{1,0:T(8,128)(2,1)} %get-tuple-element.189.x_ref.refs_16_, f32[1,768]{1,0:T(1,128)} %reshape.407.g_ref, f32[1,768]{1,0:T(1,128)} %reshape.408.b_ref, bf16[576,768]{1,0:T(8,128)(2,1)} %bitcast.43, ...), custom_call_target="tpu_custom_call" | custom-call | flops 4303355904 | bytes 8000000 | tf_op jit(solution)/shard_map/attn_fwd/pallas_call | solution.py:89
  33.3 7.3 %attn_fwd.4 = (bf16[768,768]{1,0:T(8,128)(2,1)}, bf16[576,768]{1,0:T(8,128)(2,1)}, bf16[192,768]{1,0:T(8,128)(2,1)}, f32[3,768]{1,0:T(4,128)}) custom-call(bf16[768,768]{1,0:T(8,128)(2,1)} %get-tuple-element.190.x_ref.refs_10_, f32[1,768]{1,0:T(1,128)} %reshape.407.g_ref, f32[1,768]{1,0:T(1,128)} %reshape.408.b_ref, bf16[576,768]{1,0:T(8,128)(2,1)} %bitcast.44, ...), custom_call_target="tpu_custom_call" | custom-call | flops 4303355904 | bytes 8000000 | tf_op jit(solution)/shard_map/attn_fwd/pallas_call | solution.py:89
  40.6 2.0 collective-permute-start.6
  42.7 12.8 %collective-permute-done.12.pair_ref = bf16[192,768]{1,0:T(8,128)(2,1)S(1)} collective-permute-done((bf16[192,768]{1,0:T(8,128)(2,1)}, bf16[192,768]{1,0:T(8,128)(2,1)S(1)}, u32[]{:S(2)}, u32[]{:S(2)}) %collective-permute-start.12) | collective-permute-done | bytes 294944 | tf_op jit(solution)/shard_map/ppermute | solution.py:425
  58.4 2.1 pad_maximum_fusion.1
  62.0 4.9 collective-permute-done.6.pair_ref
  66.9 1.8 pad_maximum_fusion.2
  72.1 1.6 squeeze.76.eid_ref.refs_4_
  77.6 1.6 squeeze.77.eid_ref.refs_9_
  84.2 1.8 fusion.7
  88.8 2.9 gather_fusion
  91.7 16.2 %expert_fwd_bwd.5 = (f32[768,768]{1,0:T(8,128)}, bf16[768,768]{1,0:T(8,128)(2,1)}, bf16[768,768]{1,0:T(8,128)(2,1)}, bf16[768,768]{1,0:T(8,128)(2,1)}, bf16[768,...) custom-call(s32[12]{0:T(128)} %squeeze.68.flags_ref, ...), custom_call_target="tpu_custom_call" | custom-call | flops 6704175616 | bytes 22000000 | tf_op jit(solution)/shard_map/expert_fwd_bwd/pallas_call | solution.py:168
  107.9 18.1 %collective-permute-start.30 = (bf16[672,768]{1,0:T(8,128)(2,1)}, bf16[672,768]{1,0:T(8,128)(2,1)S(1)}, u32[]{:S(2)}, u32[]{:S(2)}) collective-permute-start(bf16[672,768]{1,0:T(8,128)(2,1)} %get-tuple-element.86), channel_id=1, source_target_pairs={{0,1},{3,2},{4,5},{7,6},{8,9},{11,10},{12,13},{15,14},{16,17},{19,... | collective-permute-start | bytes 3096584 | tf_op jit(solution)/shard_map/ppermute | solution.py:413
  126.0 16.2 %expert_fwd_bwd.4 = (f32[768,768]{1,0:T(8,128)}, bf16[768,768]{1,0:T(8,128)(2,1)}, bf16[768,768]{1,0:T(8,128)(2,1)}, bf16[768,768]{1,0:T(8,128)(2,1)}, bf16[768,...) custom-call(s32[12]{0:T(128)} %squeeze.65.flags_ref, ...), custom_call_target="tpu_custom_call" | custom-call | flops 6704175616 | bytes 22000000 | tf_op jit(solution)/shard_map/expert_fwd_bwd/pallas_call | solution.py:168
  142.3 1.6 collective-permute-start.24
  143.9 16.5 %expert_fwd_bwd.3 = (f32[768,768]{1,0:T(8,128)}, bf16[768,768]{1,0:T(8,128)(2,1)}, bf16[768,768]{1,0:T(8,128)(2,1)}, bf16[768,768]{1,0:T(8,128)(2,1)}, bf16[768,...) custom-call(s32[12]{0:T(128)} %squeeze.60.flags_ref, ...), custom_call_target="tpu_custom_call" | custom-call | flops 6704175616 | bytes 22000000 | tf_op jit(solution)/shard_map/expert_fwd_bwd/pallas_call | solution.py:168
  164.3 1.7 fusion.6
  168.5 3.1 collective-permute-done.24
  172.6 20.0 %collective-permute-done.18 = bf16[672,768]{1,0:T(8,128)(2,1)S(1)} collective-permute-done((bf16[672,768]{1,0:T(8,128)(2,1)}, bf16[672,768]{1,0:T(8,128)(2,1)S(1)}, u32[]{:S(2)}, u32[]{:S(2)}) %collective-permute-start.18) | collective-permute-done | bytes 1032224 | tf_op jit(solution)/shard_map/ppermute | solution.py:413
  193.0 1.6 collective-permute-start.19
  195.6 6.1 mid_back.5
  206.4 6.2 mid_back.4
  216.2 6.0 mid_back.3
  223.5 7.1 %collective-permute-done.32.far_ref = bf16[672,768]{1,0:T(8,128)(2,1)} collective-permute-done((bf16[672,768]{1,0:T(8,128)(2,1)}, bf16[672,768]{1,0:T(8,128)(2,1)}, u32[]{:S(2)}, u32[]{:S(2)}) %collective-permute-start.32) | collective-permute-done | bytes 1032224 | tf_op jit(solution)/shard_map/ppermute | solution.py:421
  230.6 10.4 %attn_bwd.5 = (bf16[768,768]{1,0:T(8,128)(2,1)}, bf16[576,768]{1,0:T(8,128)(2,1)}, bf16[672,768]{1,0:T(8,128)(2,1)}) custom-call(s32[1]{0:T(128)} %bitcast.13.flag_ref, bf16[672,768]{1,0:T(8,128)(2,1)} %get-tuple-element.87.ga_ref, bf16[672,768]{1,0:T(8,128)(2,1)} %collective-permute-done.32.far_ref, bf16[192,768]{1,0:T(8,128)(2,1)} %wo_ref.5, ...), custom_call_target="tpu_custom_call" | custom-call | flops 8153726976 | bytes 9000000 | tf_op jit(solution)/shard_map/attn_bwd/pallas_call | solution.py:309
  240.9 11.8 %collective-permute-done.26.far_ref = bf16[672,768]{1,0:T(8,128)(2,1)} collective-permute-done((bf16[672,768]{1,0:T(8,128)(2,1)}, bf16[672,768]{1,0:T(8,128)(2,1)}, u32[]{:S(2)}, u32[]{:S(2)}) %collective-permute-start.26) | collective-permute-done | bytes 1032224 | tf_op jit(solution)/shard_map/ppermute | solution.py:421
  252.7 10.0 %attn_bwd.4 = (bf16[768,768]{1,0:T(8,128)(2,1)}, bf16[576,768]{1,0:T(8,128)(2,1)}, bf16[672,768]{1,0:T(8,128)(2,1)}) custom-call(s32[1]{0:T(128)} %bitcast.13.flag_ref, bf16[672,768]{1,0:T(8,128)(2,1)} %get-tuple-element.81.ga_ref, bf16[672,768]{1,0:T(8,128)(2,1)} %collective-permute-done.26.far_ref, bf16[192,768]{1,0:T(8,128)(2,1)} %wo_ref.5, ...), custom_call_target="tpu_custom_call" | custom-call | flops 8153726976 | bytes 9000000 | tf_op jit(solution)/shard_map/attn_bwd/pallas_call | solution.py:309
  262.7 10.2 %collective-permute-done.20.far_ref = bf16[672,768]{1,0:T(8,128)(2,1)S(1)} collective-permute-done((bf16[672,768]{1,0:T(8,128)(2,1)}, bf16[672,768]{1,0:T(8,128)(2,1)S(1)}, u32[]{:S(2)}, u32[]{:S(2)}) %collective-permute-start.20) | collective-permute-done | bytes 1032224 | tf_op jit(solution)/shard_map/ppermute | solution.py:421
  273.9 10.2 %attn_bwd.3 = (bf16[768,768]{1,0:T(8,128)(2,1)}, bf16[576,768]{1,0:T(8,128)(2,1)}, bf16[672,768]{1,0:T(8,128)(2,1)}) custom-call(s32[1]{0:T(128)} %bitcast.13.flag_ref, bf16[672,768]{1,0:T(8,128)(2,1)} %get-tuple-element.75.ga_ref, bf16[672,768]{1,0:T(8,128)(2,1)} %copy-done.44, bf16[192,768]{1,0:T(8,128)(2,1)} %wo_ref.5, ...), custom_call_target="tpu_custom_call" | custom-call | flops 8153726976 | bytes 9000000 | tf_op jit(solution)/shard_map/attn_bwd/pallas_call | solution.py:309
  284.0 12.0 %attn_grads.1 = (bf16[768,768]{1,0:T(8,128)(2,1)}, f32[8,768]{1,0:T(8,128)}, f32[576,1]{1,0:T(8,128)}) custom-call(bf16[768,768]{1,0:T(8,128)(2,1)} %get-tuple-element.95.refs_0_, bf16[576,768]{1,0:T(8,128)(2,1)} %get-tuple-element.96.refs_1_, bf16[192,768]{1,0:T(8,128)(2,1)} %get-tuple-element.65.own_ref.mix_ref.refs_2_, ...), custom_call_target="tpu_custom_call" | custom-call | flops 2717908992 | bytes 18000000 | tf_op jit(solution)/shard_map/attn_grads/pallas_call | solution.py:356
  297.3 21.2 %expert_grads.1 = bf16[768,4608]{1,0:T(8,128)(2,1)} custom-call(s32[36]{0:T(128)} %reshape.423.flags_ref, bf16[768,768]{1,0:T(8,128)(2,1)} %get-tuple-element.107.refs_0_, bf16[768,768]{1,0:T(8,128)(2,1)} %get-tuple-element.108.refs_1_, bf16[768,768]{1,0:T(8,128)(2,1)} %get-tuple-element.109.refs_2_, bf16[768,768]{1,0:T(8,128)(2,1)} %get-tuple-element.185.cot_ref.refs_3_, ...), custom_call_target="tpu_custom_call" | custom-call | flops 8153726976 | bytes 22000000 | tf_op jit(solution)/shard_map/expert_grads/pallas_call | solution.py:224
  324.0 23.5 %collective-permute-done.3 = bf16[768,768]{1,0:T(8,128)(2,1)S(1)} collective-permute-done((bf16[768,768]{1,0:T(8,128)(2,1)S(1)}, bf16[768,768]{1,0:T(8,128)(2,1)S(1)}, u32[]{:S(2)}, u32[]{:S(2)}) %collective-permute-start.3) | collective-permute-done | bytes 1179680 | tf_op jit(solution)/shard_map/ppermute | solution.py:413
  348.9 1.7 collective-permute-start.4
  350.6 22.2 %collective-permute-done.9 = bf16[768,768]{1,0:T(8,128)(2,1)S(1)} collective-permute-done((bf16[768,768]{1,0:T(8,128)(2,1)S(1)}, bf16[768,768]{1,0:T(8,128)(2,1)S(1)}, u32[]{:S(2)}, u32[]{:S(2)}) %collective-permute-start.9) | collective-permute-done | bytes 1179680 | tf_op jit(solution)/shard_map/ppermute | solution.py:413
  374.2 1.8 collective-permute-start.10
  376.0 22.1 %collective-permute-done.15 = bf16[768,768]{1,0:T(8,128)(2,1)S(1)} collective-permute-done((bf16[768,768]{1,0:T(8,128)(2,1)}, bf16[768,768]{1,0:T(8,128)(2,1)S(1)}, u32[]{:S(2)}, u32[]{:S(2)}) %collective-permute-start.15) | collective-permute-done | bytes 1179680 | tf_op jit(solution)/shard_map/ppermute | solution.py:413
  398.1 2.7 add_convert_fusion.s_ref
  400.8 1.7 collective-permute-start.16
  402.5 1.7 fusion.5
  404.3 6.3 %collective-permute-start.21 = (bf16[672,768]{1,0:T(8,128)(2,1)}, bf16[672,768]{1,0:T(8,128)(2,1)}, u32[]{:S(2)}, u32[]{:S(2)}) collective-permute-start(bf16[672,768]{1,0:T(8,128)(2,1)} %get-tuple-element.78.refs_5_), channel_id=1, source_target_pairs={{0,1},{3,2},{4,5},{7,6},{8,9},{11,10},{12,13},{15,14},{16,17},{19,... | collective-permute-start | bytes 3096584 | tf_op jit(solution)/shard_map/ppermute | solution.py:413
  410.6 4.4 layer_out_rows.3
  416.3 4.5 layer_out_rows.4
  422.3 4.5 layer_out_rows.5
  426.9 13.9 %collective-permute-start.33 = (bf16[672,768]{1,0:T(8,128)(2,1)S(1)}, bf16[672,768]{1,0:T(8,128)(2,1)}, u32[]{:S(2)}, u32[]{:S(2)}) collective-permute-start(bf16[672,768]{1,0:T(8,128)(2,1)S(1)} %copy-done.9), channel_id=1, source_target_pairs={{0,1},{3,2},{4,5},{7,6},{8,9},{11,10},{12,13},{15,14},{16,17},{19,... | collective-permute-start | bytes 3096584 | tf_op jit(solution)/shard_map/ppermute | solution.py:413
  440.8 2.3 collective-permute-start.27
  443.2 22.3 %psum.15 = f32[2880]{0:T(1024)S(1)} all-reduce(f32[2880]{0:T(1024)S(1)} %pad_maximum_fusion.5), channel_id=1, replica_groups=mesh['dp'=8,'tensor'=4] {'dp'}, use_global_device_ids=true, to_apply=%region_3.4 | all-reduce | flops 2880 | bytes 23040 | tf_op jit(solution)/shard_map/psum | solution.py:527
  468.4 37.4 %psum.14 = f32[12,768]{1,0:T(8,128)S(1)} all-reduce(f32[12,768]{1,0:T(8,128)S(1)} %pad_maximum_fusion.4), channel_id=1, replica_groups=mesh['dp'=8,'tensor'=4] {'dp','tensor'}, use_global_device_ids=true, to_apply=%region_1.2 | all-reduce | flops 9216 | bytes 73728 | tf_op jit(solution)/shard_map/psum | solution.py:526
  506.4 1.6 add_convert_fusion.7.s_ref
  512.2 1.6 collective-permute-start.28
  516.8 1.6 collective-permute-start.34
  519.4 4.9 first_back.3
  527.0 13.4 %collective-permute-done.17 = bf16[768,768]{1,0:T(8,128)(2,1)} collective-permute-done((bf16[768,768]{1,0:T(8,128)(2,1)S(1)}, bf16[768,768]{1,0:T(8,128)(2,1)}, u32[]{:S(2)}, u32[]{:S(2)}) %collective-permute-start.17) | collective-permute-done | bytes 1179680 | tf_op jit(solution)/shard_map/ppermute | solution.py:421
  541.8 4.8 first_back.4
  546.6 1.5 collective-permute-start.29
  548.1 2.0 pad_maximum_fusion
  552.2 4.9 first_back.5
  559.2 6.6 %collective-permute-done.23 = bf16[672,768]{1,0:T(8,128)(2,1)} collective-permute-done((bf16[672,768]{1,0:T(8,128)(2,1)}, bf16[672,768]{1,0:T(8,128)(2,1)}, u32[]{:S(2)}, u32[]{:S(2)}) %collective-permute-start.23) | collective-permute-done | bytes 1032224 | tf_op jit(solution)/shard_map/ppermute | solution.py:421
  565.9 2.4 select_dynamic-update-slice_fusion.2
  568.9 18.9 %collective-permute-done.29 = bf16[672,768]{1,0:T(8,128)(2,1)S(1)} collective-permute-done((bf16[672,768]{1,0:T(8,128)(2,1)}, bf16[672,768]{1,0:T(8,128)(2,1)S(1)}, u32[]{:S(2)}, u32[]{:S(2)}) %collective-permute-start.29) | collective-permute-done | bytes 1032224 | tf_op jit(solution)/shard_map/ppermute | solution.py:421
  589.7 19.4 %collective-permute-done.35 = bf16[672,768]{1,0:T(8,128)(2,1)S(1)} collective-permute-done((bf16[672,768]{1,0:T(8,128)(2,1)}, bf16[672,768]{1,0:T(8,128)(2,1)S(1)}, u32[]{:S(2)}, u32[]{:S(2)}) %collective-permute-start.35) | collective-permute-done | bytes 1032224 | tf_op jit(solution)/shard_map/ppermute | solution.py:421
  611.0 2.4 reshape.425
  (229 shorter events, 85.5 us)
Async XLA Ops:
  7.2 81.6 %all-gather.3.cloned.1.call-start = ((), (), s32[]{:S(2)}) async-start(), calls=%async_computation.4 | async-start | bytes 1474560 | tf_op jit(solution)/shard_map/all_gather | solution.py:462
  22.5 36.0 %collective-permute-start = (bf16[192,768]{1,0:T(8,128)(2,1)}, bf16[192,768]{1,0:T(8,128)(2,1)}, u32[]{:S(2)}, u32[]{:S(2)}) collective-permute-start(bf16[192,768]{1,0:T(8,128)(2,1)} %get-tuple-element.65.own_ref.mix_ref.refs_2_), channel_id=1, source_target_pairs={{0,1},{1,0},{2,3},{3,2},{4,5},{5,4},{6,7},{7,6},{8,9},{9,8},{10,11... | collective-permute-start | bytes 884744 | tf_op jit(solution)/shard_map/ppermute | solution.py:425
  25.5 524.6 %reduce-scatter.3.cloned.1.call-start = ((), (), s32[]{:S(2)}) async-start(), calls=%async_computation.2 | async-start | bytes 1327104 | tf_op jit(solution)/shard_map/reduce_scatter | solution.py:513
  33.3 22.2 %collective-permute-start.12 = (bf16[192,768]{1,0:T(8,128)(2,1)}, bf16[192,768]{1,0:T(8,128)(2,1)S(1)}, u32[]{:S(2)}, u32[]{:S(2)}) collective-permute-start(bf16[192,768]{1,0:T(8,128)(2,1)} %get-tuple-element.71.own_ref.mix_ref.refs_14_), channel_id=1, source_target_pairs={{0,1},{1,0},{2,3},{3,2},{4,5},{5,4},{6,7},{7,6},{8,9},{9,8},{10,11... | collective-permute-start | bytes 884744 | tf_op jit(solution)/shard_map/ppermute | solution.py:425
  33.3 9.4 %copy-start.35 = (s32[2304]{0:T(1024)S(1)}, s32[2304]{0:T(1024)}, u32[]{:S(2)}) copy-start(s32[2304]{0:T(1024)} %param.19) | copy-start | bytes 27652
  33.3 22.2 %copy-start.23 = (bf16[192,768]{1,0:T(8,128)(2,1)S(1)}, bf16[192,768]{1,0:T(8,128)(2,1)}, u32[]{:S(2)}) copy-start(bf16[192,768]{1,0:T(8,128)(2,1)} %get-tuple-element.71.own_ref.mix_ref.refs_14_) | copy-start | bytes 884740
  40.6 26.3 %collective-permute-start.6 = (bf16[192,768]{1,0:T(8,128)(2,1)}, bf16[192,768]{1,0:T(8,128)(2,1)}, u32[]{:S(2)}, u32[]{:S(2)}) collective-permute-start(bf16[192,768]{1,0:T(8,128)(2,1)} %get-tuple-element.68.own_ref.mix_ref.refs_8_), channel_id=1, source_target_pairs={{0,1},{1,0},{2,3},{3,2},{4,5},{5,4},{6,7},{7,6},{8,9},{9,8},{10,11... | collective-permute-start | bytes 884744 | tf_op jit(solution)/shard_map/ppermute | solution.py:425
  42.7 24.2 %copy-start.24 = (bf16[192,768]{1,0:T(8,128)(2,1)S(1)}, bf16[192,768]{1,0:T(8,128)(2,1)}, u32[]{:S(2)}) copy-start(bf16[192,768]{1,0:T(8,128)(2,1)} %get-tuple-element.68.own_ref.mix_ref.refs_8_) | copy-start | bytes 884740
  55.6 14.6 %collective-permute-start.13 = (bf16[384,768]{1,0:T(8,128)(2,1)S(1)}, bf16[384,768]{1,0:T(8,128)(2,1)}, u32[]{:S(2)}, u32[]{:S(2)}) collective-permute-start(bf16[384,768]{1,0:T(8,128)(2,1)S(1)} %pad_maximum_fusion.3), channel_id=1, source_target_pairs={{1,2},{2,1},{5,6},{6,5},{9,10},{10,9},{13,14},{14,13},{17,18},{18,... | collective-permute-start | bytes 1769480 | tf_op jit(solution)/shard_map/ppermute | solution.py:417
  58.4 25.8 %copy-start = (bf16[2304,768]{1,0:T(8,128)(2,1)S(1)}, bf16[2304,768]{1,0:T(8,128)(2,1)}, u32[]{:S(2)}) copy-start(bf16[2304,768]{1,0:T(8,128)(2,1)} %param.18) | copy-start | bytes 10616836
  60.5 25.5 %collective-permute-start.1 = (bf16[384,768]{1,0:T(8,128)(2,1)}, bf16[384,768]{1,0:T(8,128)(2,1)}, u32[]{:S(2)}, u32[]{:S(2)}) collective-permute-start(bf16[384,768]{1,0:T(8,128)(2,1)} %pad_maximum_fusion.1), channel_id=1, source_target_pairs={{1,2},{2,1},{5,6},{6,5},{9,10},{10,9},{13,14},{14,13},{17,18},{18,... | collective-permute-start | bytes 1769480 | tf_op jit(solution)/shard_map/ppermute | solution.py:417
  68.7 18.6 %collective-permute-start.7 = (bf16[384,768]{1,0:T(8,128)(2,1)}, bf16[384,768]{1,0:T(8,128)(2,1)}, u32[]{:S(2)}, u32[]{:S(2)}) collective-permute-start(bf16[384,768]{1,0:T(8,128)(2,1)} %pad_maximum_fusion.2), channel_id=1, source_target_pairs={{1,2},{2,1},{5,6},{6,5},{9,10},{10,9},{13,14},{14,13},{17,18},{18,... | collective-permute-start | bytes 1769480 | tf_op jit(solution)/shard_map/ppermute | solution.py:417
  70.2 21.5 %collective-permute-start.14 = (bf16[384,768]{1,0:T(8,128)(2,1)}, bf16[384,768]{1,0:T(8,128)(2,1)}, u32[]{:S(2)}, u32[]{:S(2)}) collective-permute-start(bf16[384,768]{1,0:T(8,128)(2,1)} %collective-permute-done.13.far_a_ref), channel_id=1, source_target_pairs={{1,0},{2,3},{5,4},{6,7},{9,8},{10,11},{13,12},{14,15},{17,16},{18,... | collective-permute-start | bytes 1769480 | tf_op jit(solution)/shard_map/ppermute | solution.py:421
  86.0 57.8 %collective-permute-start.2 = (bf16[384,768]{1,0:T(8,128)(2,1)}, bf16[384,768]{1,0:T(8,128)(2,1)}, u32[]{:S(2)}, u32[]{:S(2)}) collective-permute-start(bf16[384,768]{1,0:T(8,128)(2,1)} %collective-permute-done.1.far_a_ref), channel_id=1, source_target_pairs={{1,0},{2,3},{5,4},{6,7},{9,8},{10,11},{13,12},{14,15},{17,16},{18,... | collective-permute-start | bytes 1769480 | tf_op jit(solution)/shard_map/ppermute | solution.py:421
  87.3 38.7 %collective-permute-start.8 = (bf16[384,768]{1,0:T(8,128)(2,1)}, bf16[384,768]{1,0:T(8,128)(2,1)}, u32[]{:S(2)}, u32[]{:S(2)}) collective-permute-start(bf16[384,768]{1,0:T(8,128)(2,1)} %collective-permute-done.7.far_a_ref), channel_id=1, source_target_pairs={{1,0},{2,3},{5,4},{6,7},{9,8},{10,11},{13,12},{14,15},{17,16},{18,... | collective-permute-start | bytes 1769480 | tf_op jit(solution)/shard_map/ppermute | solution.py:421
  107.9 53.9 %collective-permute-start.30 = (bf16[672,768]{1,0:T(8,128)(2,1)}, bf16[672,768]{1,0:T(8,128)(2,1)S(1)}, u32[]{:S(2)}, u32[]{:S(2)}) collective-permute-start(bf16[672,768]{1,0:T(8,128)(2,1)} %get-tuple-element.86), channel_id=1, source_target_pairs={{0,1},{3,2},{4,5},{7,6},{8,9},{11,10},{12,13},{15,14},{16,17},{19,... | collective-permute-start | bytes 3096584 | tf_op jit(solution)/shard_map/ppermute | solution.py:413
  142.3 29.3 %collective-permute-start.24 = (bf16[672,768]{1,0:T(8,128)(2,1)}, bf16[672,768]{1,0:T(8,128)(2,1)S(1)}, u32[]{:S(2)}, u32[]{:S(2)}) collective-permute-start(bf16[672,768]{1,0:T(8,128)(2,1)} %get-tuple-element.80), channel_id=1, source_target_pairs={{0,1},{3,2},{4,5},{7,6},{8,9},{11,10},{12,13},{15,14},{16,17},{19,... | collective-permute-start | bytes 3096584 | tf_op jit(solution)/shard_map/ppermute | solution.py:413
  143.9 17.9 %copy-start.27 = (bf16[672,768]{1,0:T(8,128)(2,1)S(1)}, bf16[672,768]{1,0:T(8,128)(2,1)}, u32[]{:S(2)}) copy-start(bf16[672,768]{1,0:T(8,128)(2,1)} %get-tuple-element.86) | copy-start | bytes 3096580
  160.4 32.2 %collective-permute-start.18 = (bf16[672,768]{1,0:T(8,128)(2,1)}, bf16[672,768]{1,0:T(8,128)(2,1)S(1)}, u32[]{:S(2)}, u32[]{:S(2)}) collective-permute-start(bf16[672,768]{1,0:T(8,128)(2,1)} %get-tuple-element.74), channel_id=1, source_target_pairs={{0,1},{3,2},{4,5},{7,6},{8,9},{11,10},{12,13},{15,14},{16,17},{19,... | collective-permute-start | bytes 3096584 | tf_op jit(solution)/shard_map/ppermute | solution.py:413
  162.1 32.5 %collective-permute-start.31 = (bf16[672,768]{1,0:T(8,128)(2,1)S(1)}, bf16[672,768]{1,0:T(8,128)(2,1)S(1)}, u32[]{:S(2)}, u32[]{:S(2)}) collective-permute-start(bf16[672,768]{1,0:T(8,128)(2,1)S(1)} %add_convert_fusion.4.s_ref), channel_id=1, source_target_pairs={{1,2},{2,1},{5,6},{6,5},{9,10},{10,9},{13,14},{14,13},{17,18},{18,... | collective-permute-start | bytes 3096584 | tf_op jit(solution)/shard_map/ppermute | solution.py:417
  167.1 4.5 copy-start.26
  168.5 24.2 %copy-start.28 = (bf16[672,768]{1,0:T(8,128)(2,1)S(1)}, bf16[672,768]{1,0:T(8,128)(2,1)}, u32[]{:S(2)}) copy-start(bf16[672,768]{1,0:T(8,128)(2,1)} %get-tuple-element.74) | copy-start | bytes 3096580
  171.9 21.1 %copy-start.20 = (bf16[672,768]{1,0:T(8,128)(2,1)}, bf16[672,768]{1,0:T(8,128)(2,1)S(1)}, u32[]{:S(2)}) copy-start(bf16[672,768]{1,0:T(8,128)(2,1)S(1)} %add_convert_fusion.6.s_ref) | copy-start | bytes 3096580
  171.9 33.5 %collective-permute-start.25 = (bf16[672,768]{1,0:T(8,128)(2,1)S(1)}, bf16[672,768]{1,0:T(8,128)(2,1)S(1)}, u32[]{:S(2)}, u32[]{:S(2)}) collective-permute-start(bf16[672,768]{1,0:T(8,128)(2,1)S(1)} %add_convert_fusion.6.s_ref), channel_id=1, source_target_pairs={{1,2},{2,1},{5,6},{6,5},{9,10},{10,9},{13,14},{14,13},{17,18},{18,... | collective-permute-start | bytes 3096584 | tf_op jit(solution)/shard_map/ppermute | solution.py:417
  192.9 8.8 %copy-start.18 = (bf16[672,768]{1,0:T(8,128)(2,1)}, bf16[672,768]{1,0:T(8,128)(2,1)S(1)}, u32[]{:S(2)}) copy-start(bf16[672,768]{1,0:T(8,128)(2,1)S(1)} %add_convert_fusion.8.s_ref) | copy-start | bytes 3096580
  193.0 23.2 %collective-permute-start.19 = (bf16[672,768]{1,0:T(8,128)(2,1)S(1)}, bf16[672,768]{1,0:T(8,128)(2,1)}, u32[]{:S(2)}, u32[]{:S(2)}) collective-permute-start(bf16[672,768]{1,0:T(8,128)(2,1)S(1)} %add_convert_fusion.8.s_ref), channel_id=1, source_target_pairs={{1,2},{2,1},{5,6},{6,5},{9,10},{10,9},{13,14},{14,13},{17,18},{18,... | collective-permute-start | bytes 3096584 | tf_op jit(solution)/shard_map/ppermute | solution.py:417
  195.6 7.4 %copy-start.39 = (s32[672]{0:T(1024)S(1)}, s32[672]{0:T(1024)}, u32[]{:S(2)}) copy-start(s32[672]{0:T(1024)} %get-tuple-element.205) | copy-start | bytes 8068
  195.6 8.3 %copy-start.4 = (f32[768,768]{1,0:T(8,128)S(1)}, f32[768,768]{1,0:T(8,128)}, u32[]{:S(2)}) copy-start(f32[768,768]{1,0:T(8,128)} %get-tuple-element.70.mid_ref) | copy-start | bytes 7077892
  201.7 28.8 %collective-permute-start.32 = (bf16[672,768]{1,0:T(8,128)(2,1)}, bf16[672,768]{1,0:T(8,128)(2,1)}, u32[]{:S(2)}, u32[]{:S(2)}) collective-permute-start(bf16[672,768]{1,0:T(8,128)(2,1)} %get-tuple-element.87.ga_ref), channel_id=1, source_target_pairs={{1,0},{2,3},{5,4},{6,7},{9,8},{10,11},{13,12},{14,15},{17,16},{18,... | collective-permute-start | bytes 3096584 | tf_op jit(solution)/shard_map/ppermute | solution.py:421
  206.4 8.4 %copy-start.5 = (f32[768,768]{1,0:T(8,128)S(1)}, f32[768,768]{1,0:T(8,128)}, u32[]{:S(2)}) copy-start(f32[768,768]{1,0:T(8,128)} %get-tuple-element.67.mid_ref) | copy-start | bytes 7077892
  212.5 40.1 %collective-permute-start.26 = (bf16[672,768]{1,0:T(8,128)(2,1)}, bf16[672,768]{1,0:T(8,128)(2,1)}, u32[]{:S(2)}, u32[]{:S(2)}) collective-permute-start(bf16[672,768]{1,0:T(8,128)(2,1)} %get-tuple-element.81.ga_ref), channel_id=1, source_target_pairs={{1,0},{2,3},{5,4},{6,7},{9,8},{10,11},{13,12},{14,15},{17,16},{18,... | collective-permute-start | bytes 3096584 | tf_op jit(solution)/shard_map/ppermute | solution.py:421
  222.2 50.7 %collective-permute-start.20 = (bf16[672,768]{1,0:T(8,128)(2,1)}, bf16[672,768]{1,0:T(8,128)(2,1)S(1)}, u32[]{:S(2)}, u32[]{:S(2)}) collective-permute-start(bf16[672,768]{1,0:T(8,128)(2,1)} %get-tuple-element.75.ga_ref), channel_id=1, source_target_pairs={{1,0},{2,3},{5,4},{6,7},{9,8},{10,11},{13,12},{14,15},{17,16},{18,... | collective-permute-start | bytes 3096584 | tf_op jit(solution)/shard_map/ppermute | solution.py:421
  296.0 315.0 %reduce-scatter.5.cloned.1.call-start = ((), (), s32[]{:S(2)}) async-start(), calls=%async_computation.3 | async-start | bytes 7962624 | tf_op jit(solution)/shard_map/reduce_scatter | solution.py:510
  319.8 27.7 %collective-permute-start.3 = (bf16[768,768]{1,0:T(8,128)(2,1)S(1)}, bf16[768,768]{1,0:T(8,128)(2,1)S(1)}, u32[]{:S(2)}, u32[]{:S(2)}) collective-permute-start(bf16[768,768]{1,0:T(8,128)(2,1)S(1)} %copy-done.22), channel_id=1, source_target_pairs={{0,1},{3,2},{4,5},{7,6},{8,9},{11,10},{12,13},{15,14},{16,17},{19,... | collective-permute-start | bytes 3538952 | tf_op jit(solution)/shard_map/ppermute | solution.py:413
  321.3 51.5 %collective-permute-start.9 = (bf16[768,768]{1,0:T(8,128)(2,1)S(1)}, bf16[768,768]{1,0:T(8,128)(2,1)S(1)}, u32[]{:S(2)}, u32[]{:S(2)}) collective-permute-start(bf16[768,768]{1,0:T(8,128)(2,1)S(1)} %copy-done.21), channel_id=1, source_target_pairs={{0,1},{3,2},{4,5},{7,6},{8,9},{11,10},{12,13},{15,14},{16,17},{19,... | collective-permute-start | bytes 3538952 | tf_op jit(solution)/shard_map/ppermute | solution.py:413
  322.6 75.5 %collective-permute-start.15 = (bf16[768,768]{1,0:T(8,128)(2,1)}, bf16[768,768]{1,0:T(8,128)(2,1)S(1)}, u32[]{:S(2)}, u32[]{:S(2)}) collective-permute-start(bf16[768,768]{1,0:T(8,128)(2,1)} %get-tuple-element.72), channel_id=1, source_target_pairs={{0,1},{3,2},{4,5},{7,6},{8,9},{11,10},{12,13},{15,14},{16,17},{19,... | collective-permute-start | bytes 3538952 | tf_op jit(solution)/shard_map/ppermute | solution.py:413
  348.9 61.7 %collective-permute-start.4 = (bf16[768,768]{1,0:T(8,128)(2,1)}, bf16[768,768]{1,0:T(8,128)(2,1)}, u32[]{:S(2)}, u32[]{:S(2)}) collective-permute-start(bf16[768,768]{1,0:T(8,128)(2,1)} %add_convert_fusion.2.s_ref), channel_id=1, source_target_pairs={{1,2},{2,1},{5,6},{6,5},{9,10},{10,9},{13,14},{14,13},{17,18},{18,... | collective-permute-start | bytes 3538952 | tf_op jit(solution)/shard_map/ppermute | solution.py:417
  374.2 28.3 %copy-start.2 = (bf16[2304,768]{1,0:T(8,128)(2,1)S(1)}, bf16[2304,768]{1,0:T(8,128)(2,1)}, u32[]{:S(2)}) copy-start(bf16[2304,768]{1,0:T(8,128)(2,1)} %param.17) | copy-start | bytes 10616836
  374.2 42.1 %collective-permute-start.10 = (bf16[768,768]{1,0:T(8,128)(2,1)}, bf16[768,768]{1,0:T(8,128)(2,1)}, u32[]{:S(2)}, u32[]{:S(2)}) collective-permute-start(bf16[768,768]{1,0:T(8,128)(2,1)} %add_convert_fusion.1.s_ref), channel_id=1, source_target_pairs={{1,2},{2,1},{5,6},{6,5},{9,10},{10,9},{13,14},{14,13},{17,18},{18,... | collective-permute-start | bytes 3538952 | tf_op jit(solution)/shard_map/ppermute | solution.py:417
  400.8 21.5 %collective-permute-start.16 = (bf16[768,768]{1,0:T(8,128)(2,1)}, bf16[768,768]{1,0:T(8,128)(2,1)}, u32[]{:S(2)}, u32[]{:S(2)}) collective-permute-start(bf16[768,768]{1,0:T(8,128)(2,1)} %add_convert_fusion.s_ref), channel_id=1, source_target_pairs={{1,2},{2,1},{5,6},{6,5},{9,10},{10,9},{13,14},{14,13},{17,18},{18,... | collective-permute-start | bytes 3538952 | tf_op jit(solution)/shard_map/ppermute | solution.py:417
  404.3 10.8 %copy-start.34 = (f32[12,768]{1,0:T(8,128)}, f32[12,768]{1,0:T(8,128)S(1)}, u32[]{:S(2)}) copy-start(f32[12,768]{1,0:T(8,128)S(1)} %add_add_fusion) | copy-start | bytes 110596
  404.3 102.1 %collective-permute-start.21 = (bf16[672,768]{1,0:T(8,128)(2,1)}, bf16[672,768]{1,0:T(8,128)(2,1)}, u32[]{:S(2)}, u32[]{:S(2)}) collective-permute-start(bf16[672,768]{1,0:T(8,128)(2,1)} %get-tuple-element.78.refs_5_), channel_id=1, source_target_pairs={{0,1},{3,2},{4,5},{7,6},{8,9},{11,10},{12,13},{15,14},{16,17},{19,... | collective-permute-start | bytes 3096584 | tf_op jit(solution)/shard_map/ppermute | solution.py:413
  415.0 97.2 %collective-permute-start.5 = (bf16[768,768]{1,0:T(8,128)(2,1)}, bf16[768,768]{1,0:T(8,128)(2,1)}, u32[]{:S(2)}, u32[]{:S(2)}) collective-permute-start(bf16[768,768]{1,0:T(8,128)(2,1)} %layer_out_rows.3), channel_id=1, source_target_pairs={{1,0},{2,3},{5,4},{6,7},{9,8},{10,11},{13,12},{14,15},{17,16},{18,... | collective-permute-start | bytes 3538952 | tf_op jit(solution)/shard_map/ppermute | solution.py:421
  420.9 6.0 copy-start.9
  420.9 19.9 %copy-start.10 = (bf16[672,768]{1,0:T(8,128)(2,1)S(1)}, bf16[672,768]{1,0:T(8,128)(2,1)}, u32[]{:S(2)}) copy-start(bf16[672,768]{1,0:T(8,128)(2,1)} %get-tuple-element.84.refs_11_) | copy-start | bytes 3096580
  420.9 22.2 %copy-start.32 = (f32[576,1]{1,0:T(8,128)S(1)}, f32[576,1]{1,0:T(8,128)}, u32[]{:S(2)}) copy-start(f32[576,1]{1,0:T(8,128)} %get-tuple-element.106) | copy-start | bytes 6916
  420.9 47.5 %slice-start = ((f32[12,768]{1,0:T(8,128)}), f32[6,768]{1,0:T(8,128)S(1)}, s32[]{:S(2)}) async-start(f32[12,768]{1,0:T(8,128)} %copy-done.34), calls=%async_computation.5 | async-start | bytes 49152 | tf_op jit(solution)/shard_map/slice | solution.py:519
  420.9 104.7 %collective-permute-start.11 = (bf16[768,768]{1,0:T(8,128)(2,1)}, bf16[768,768]{1,0:T(8,128)(2,1)}, u32[]{:S(2)}, u32[]{:S(2)}) collective-permute-start(bf16[768,768]{1,0:T(8,128)(2,1)} %layer_out_rows.4), channel_id=1, source_target_pairs={{1,0},{2,3},{5,4},{6,7},{9,8},{10,11},{13,12},{14,15},{17,16},{18,... | collective-permute-start | bytes 3538952 | tf_op jit(solution)/shard_map/ppermute | solution.py:421
  422.3 84.1 %copy-start.11 = (bf16[672,768]{1,0:T(8,128)(2,1)S(1)}, bf16[672,768]{1,0:T(8,128)(2,1)}, u32[]{:S(2)}) copy-start(bf16[672,768]{1,0:T(8,128)(2,1)} %get-tuple-element.78.refs_5_) | copy-start | bytes 3096580
  426.9 88.4 %collective-permute-start.33 = (bf16[672,768]{1,0:T(8,128)(2,1)S(1)}, bf16[672,768]{1,0:T(8,128)(2,1)}, u32[]{:S(2)}, u32[]{:S(2)}) collective-permute-start(bf16[672,768]{1,0:T(8,128)(2,1)S(1)} %copy-done.9), channel_id=1, source_target_pairs={{0,1},{3,2},{4,5},{7,6},{8,9},{11,10},{12,13},{15,14},{16,17},{19,... | collective-permute-start | bytes 3096584 | tf_op jit(solution)/shard_map/ppermute | solution.py:413
  440.8 68.6 %collective-permute-start.27 = (bf16[672,768]{1,0:T(8,128)(2,1)S(1)}, bf16[672,768]{1,0:T(8,128)(2,1)}, u32[]{:S(2)}, u32[]{:S(2)}) collective-permute-start(bf16[672,768]{1,0:T(8,128)(2,1)S(1)} %copy-done.10), channel_id=1, source_target_pairs={{0,1},{3,2},{4,5},{7,6},{8,9},{11,10},{12,13},{15,14},{16,17},{19,... | collective-permute-start | bytes 3096584 | tf_op jit(solution)/shard_map/ppermute | solution.py:413
  508.0 10.5 %collective-permute-start.22 = (bf16[672,768]{1,0:T(8,128)(2,1)S(1)}, bf16[672,768]{1,0:T(8,128)(2,1)S(1)}, u32[]{:S(2)}, u32[]{:S(2)}) collective-permute-start(bf16[672,768]{1,0:T(8,128)(2,1)S(1)} %add_convert_fusion.7.s_ref), channel_id=1, source_target_pairs={{1,2},{2,1},{5,6},{6,5},{9,10},{10,9},{13,14},{14,13},{17,18},{18,... | collective-permute-start | bytes 3096584 | tf_op jit(solution)/shard_map/ppermute | solution.py:417
  509.3 4.6 copy-start.8
  509.3 31.0 %collective-permute-start.17 = (bf16[768,768]{1,0:T(8,128)(2,1)S(1)}, bf16[768,768]{1,0:T(8,128)(2,1)}, u32[]{:S(2)}, u32[]{:S(2)}) collective-permute-start(bf16[768,768]{1,0:T(8,128)(2,1)S(1)} %copy-done.7), channel_id=1, source_target_pairs={{1,0},{2,3},{5,4},{6,7},{9,8},{10,11},{13,12},{14,15},{17,16},{18,... | collective-permute-start | bytes 3538952 | tf_op jit(solution)/shard_map/ppermute | solution.py:421
  512.2 29.5 %collective-permute-start.28 = (bf16[672,768]{1,0:T(8,128)(2,1)S(1)}, bf16[672,768]{1,0:T(8,128)(2,1)}, u32[]{:S(2)}, u32[]{:S(2)}) collective-permute-start(bf16[672,768]{1,0:T(8,128)(2,1)S(1)} %add_convert_fusion.5.s_ref), channel_id=1, source_target_pairs={{1,2},{2,1},{5,6},{6,5},{9,10},{10,9},{13,14},{14,13},{17,18},{18,... | collective-permute-start | bytes 3096584 | tf_op jit(solution)/shard_map/ppermute | solution.py:417
  516.8 7.5 %copy-start.13 = (bf16[672,768]{1,0:T(8,128)(2,1)}, bf16[672,768]{1,0:T(8,128)(2,1)S(1)}, u32[]{:S(2)}) copy-start(bf16[672,768]{1,0:T(8,128)(2,1)S(1)} %add_convert_fusion.3.s_ref) | copy-start | bytes 3096580
  516.8 35.4 %collective-permute-start.34 = (bf16[672,768]{1,0:T(8,128)(2,1)S(1)}, bf16[672,768]{1,0:T(8,128)(2,1)}, u32[]{:S(2)}, u32[]{:S(2)}) collective-permute-start(bf16[672,768]{1,0:T(8,128)(2,1)S(1)} %add_convert_fusion.3.s_ref), channel_id=1, source_target_pairs={{1,2},{2,1},{5,6},{6,5},{9,10},{10,9},{13,14},{14,13},{17,18},{18,... | collective-permute-start | bytes 3096584 | tf_op jit(solution)/shard_map/ppermute | solution.py:417
  519.4 6.2 copy-start.6
  524.3 41.6 %collective-permute-start.23 = (bf16[672,768]{1,0:T(8,128)(2,1)}, bf16[672,768]{1,0:T(8,128)(2,1)}, u32[]{:S(2)}, u32[]{:S(2)}) collective-permute-start(bf16[672,768]{1,0:T(8,128)(2,1)} %first_back.3), channel_id=1, source_target_pairs={{1,0},{2,3},{5,4},{6,7},{9,8},{10,11},{13,12},{14,15},{17,16},{18,... | collective-permute-start | bytes 3096584 | tf_op jit(solution)/shard_map/ppermute | solution.py:421
  546.6 41.2 %collective-permute-start.29 = (bf16[672,768]{1,0:T(8,128)(2,1)}, bf16[672,768]{1,0:T(8,128)(2,1)S(1)}, u32[]{:S(2)}, u32[]{:S(2)}) collective-permute-start(bf16[672,768]{1,0:T(8,128)(2,1)} %first_back.4), channel_id=1, source_target_pairs={{1,0},{2,3},{5,4},{6,7},{9,8},{10,11},{13,12},{14,15},{17,16},{18,... | collective-permute-start | bytes 3096584 | tf_op jit(solution)/shard_map/ppermute | solution.py:421
  552.2 13.7 %copy-start.12 = (bf16[672,768]{1,0:T(8,128)(2,1)S(1)}, bf16[672,768]{1,0:T(8,128)(2,1)}, u32[]{:S(2)}) copy-start(bf16[672,768]{1,0:T(8,128)(2,1)} %first_back.3) | copy-start | bytes 3096580
  557.1 52.0 %collective-permute-start.35 = (bf16[672,768]{1,0:T(8,128)(2,1)}, bf16[672,768]{1,0:T(8,128)(2,1)S(1)}, u32[]{:S(2)}, u32[]{:S(2)}) collective-permute-start(bf16[672,768]{1,0:T(8,128)(2,1)} %first_back.5), channel_id=1, source_target_pairs={{1,0},{2,3},{5,4},{6,7},{9,8},{10,11},{13,12},{14,15},{17,16},{18,... | collective-permute-start | bytes 3096584 | tf_op jit(solution)/shard_map/ppermute | solution.py:421
  559.2 28.6 %copy-start.15 = (bf16[672,768]{1,0:T(8,128)(2,1)S(1)}, bf16[672,768]{1,0:T(8,128)(2,1)}, u32[]{:S(2)}) copy-start(bf16[672,768]{1,0:T(8,128)(2,1)} %first_back.4) | copy-start | bytes 3096580
  568.9 40.2 %copy-start.17 = (bf16[672,768]{1,0:T(8,128)(2,1)S(1)}, bf16[672,768]{1,0:T(8,128)(2,1)}, u32[]{:S(2)}) copy-start(bf16[672,768]{1,0:T(8,128)(2,1)} %first_back.5) | copy-start | bytes 3096580
  (21 other events, 44.2 us)
Sparse Core Ops, SparseCore 0:
  25.6 43.3 all-gather.2
  296.1 35.4 reduce-scatter.2
  335.6 65.4 reduce-scatter.4
